TPU v7x, 128 devices: a whole 4x4x4 slice. The times are simulated.
128 devices in a mesh: row: 16 (over x, z_lo, core), col: 8 (over z_hi, y).
Axes of the slice: x: 4, y: 4, z: 4 (z_hi: 2, z_lo: 2; z = z_hi * 2 + z_lo), core: 2. Of those that a mesh axis runs over, the one named last changes fastest.
Arguments:
- precision: float32 [16384, 16384], P('row', 'col'), may hold values from -0.3 to 4, as said below
- samples: bfloat16 [1024, 16384], P(None, 'col'), may hold values from -6 to 6
- step_size: float32 [1], replicated, may hold values from 0.5 to 1
- threshold: float32 [1], replicated, may hold values from 0.1 to 0.3
Outputs:
- updated: float32 [16384, 16384], P('row', 'col')
Inputs may be any that keep to these rules, and one draw needn't show every extreme that they name: precision is symmetric; its diagonal entries lie between 1 and 4.
All inputs are finite; a program needn't handle non-finite values.
Results may differ from a plain program's by a relative error of at most 0.0056.
Values may be sent and summed in bfloat16 or wider, within the bound.
No kernel may reach another device: no remote copies, remote signals or barrier semaphores. Data moves between devices by JAX's collectives and lax.ppermute only.
A program may use at most 192 MiB of HBM per device.

v0:
```python
import jax
import jax.numpy as jnp
from jax import lax
from jax.sharding import Mesh
from jax.sharding import PartitionSpec as P

COL = ("col_0", "col_1")


def reduced_to_own(pieces, axes, turns):
    shape = [lax.axis_size(a) for a in axes]
    pieces = pieces.reshape(*shape, *pieces.shape[1:])
    pieces = pieces.transpose(*turns, *range(len(axes), pieces.ndim))
    pieces = pieces.reshape(-1, *pieces.shape[len(axes) :])
    for k in turns:
        pieces = lax.psum_scatter(pieces, axes[k], scatter_dimension=0, tiled=True)
    return pieces[0]


def cut_along(array, dim, length):
    shape = array.shape
    pieces = array.reshape(*shape[:dim], length, shape[dim] // length, *shape[dim + 1 :])
    return jnp.moveaxis(pieces, dim, 0)


def sum_by_axis(array, axes, turns, dim):
    length = lax.axis_size(axes)
    return reduced_to_own(cut_along(array, dim, length), axes, turns)


def sent_to_all(array, axis):
    length = lax.axis_size(axis)
    return lax.all_to_all(
        jnp.broadcast_to(array[None], (length, *array.shape)), axis, 0, 0, tiled=True
    )


def laid_out(pieces, dim):
    shape = list(pieces.shape[1:])
    shape[dim] *= pieces.shape[0]
    return jnp.moveaxis(pieces, 0, dim).reshape(shape)


def gather_directly(array, axis, dim):
    pieces = sent_to_all(array, axis)
    return laid_out(pieces, dim)


def rows_for(lines, length):
    spare = -len(lines) % length
    return jnp.pad(lines, [(0, spare)] + [(0, 0)] * (lines.ndim - 1))


def spread(array, axis, root):
    lines = jnp.where(lax.axis_index(axis) == root, array, jnp.zeros_like(array)).reshape(
        -1, *array.shape[1:][-1:]
    )
    padded = rows_for(lines, lax.axis_size(axis))
    own = lax.psum_scatter(padded, axis, scatter_dimension=0, tiled=True)
    return lax.all_gather(own, axis, axis=0, tiled=True)[: len(lines)].reshape(array.shape)


def per_device(precision, samples, step_size, threshold):
    rows_tile, cols_tile = precision.shape
    sample_count = samples.shape[0]
    col_count = lax.axis_size(COL)
    rounded = precision.astype(jnp.bfloat16)
    sample_part = samples
    projected = sum_by_axis(
        lax.dot_general(
            sample_part, rounded, (((1,), (1,)), ((), ())), preferred_element_type=jnp.float32
        ),
        COL,
        (1, 0),
        0,
    ).astype(jnp.bfloat16)
    sample_part = samples
    cross_tile = (
        lax.dot_general(
            gather_directly(projected, COL, 0),
            sample_part,
            (((0,), (0,)), ((), ())),
            preferred_element_type=jnp.float32,
        )
        / sample_count
    )
    row_index = lax.axis_index("row")
    col_index = lax.axis_index(COL)
    row_ratio = lax.axis_size("row") // col_count
    full_panel = lax.all_gather(projected, "row", axis=1, tiled=True)
    dealt = lax.all_to_all(full_panel, COL, split_axis=1, concat_axis=0, tiled=True)
    own_columns = lax.dynamic_slice_in_dim(samples, row_index % row_ratio * rows_tile, rows_tile, 1)
    own_columns = spread(own_columns, COL, row_index // row_ratio)
    mirrored = (
        lax.dot_general(
            own_columns, dealt, (((0,), (0,)), ((), ())), preferred_element_type=jnp.float32
        )
        / sample_count
    )
    symmetric = 0.5 * (cross_tile + mirrored)
    global_row = row_index * rows_tile + jnp.arange(rows_tile, dtype=jnp.int32)
    global_col = col_index * cols_tile + jnp.arange(cols_tile, dtype=jnp.int32)
    on_diagonal = global_row[:, None] == global_col[None, :]
    gradient = symmetric - jnp.where(on_diagonal, 1.0 / jnp.where(on_diagonal, precision, 1.0), 0.0)
    stepped = precision - step_size[0] * gradient
    shrunk = jnp.sign(stepped) * jnp.maximum(jnp.abs(stepped) - step_size[0] * threshold[0], 0.0)
    return jnp.where(on_diagonal, stepped, shrunk)


def solution(mesh):
    split = Mesh(mesh.devices.reshape(mesh.shape["row"], 2, 4), ("row", "col_0", "col_1"))
    placed = (P("row", COL), P(None, COL), P(), P())
    return jax.shard_map(
        per_device, mesh=split, in_specs=placed, out_specs=P("row", COL), check_vma=False
    )
```

profile of v0, /device:TPU:0, one launch (start us, length us, event | category | flops | bytes accessed | tf_op | source)
XLA Modules:
  0.0 351.2 jit_solution(9892317818716501703)
XLA Ops:
  6.5 0.0 reduce-scatter.4.cloned.1.call-start
  6.5 8.2 %fusion.4 = f32[1024,1024]{1,0:T(8,128)S(1)} fusion(bf16[1024,2048]{1,0:T(8,128)(2,1)} %param.5, f32[1024,2048]{1,0:T(8,128)} %param.4), kind=kOutput, calls=%fused_computation.7 | convolution fusion | flops 4297064448 | bytes 16777216 | tf_op jit(solution)/shard_map/dot_general | solution.py:70
  14.8 2.5 copy.5
  17.3 0.0 reduce-scatter.4.cloned.1.call-update
  17.3 0.0 reduce-scatter.6.cloned.1.call-start
  17.4 49.5 %reduce-scatter.4.cloned.1.call-done = f32[2,128,1024]{2,1,0:T(8,128)} async-done(((f32[8,128,1024]{2,1,0:T(8,128)}), f32[2,128,1024]{2,1,0:T(8,128)}) %reduce-scatter.4.cloned.1.call-update) | async-done | bytes 1048592 | tf_op jit(solution)/shard_map/reduce_scatter | solution.py:16
  66.8 0.0 reduce-scatter.6.cloned.1.call-update
  66.8 0.0 reduce-scatter.8.cloned.1.call-start
  66.9 3.4 dynamic-slice_select_fusion
  70.4 0.0 reduce-scatter.8.cloned.1.call-update
  70.4 0.0 all-gather.6.cloned.1.call-start
  70.5 23.0 %reduce-scatter.6.cloned.1.call-done = f32[1,128,1024]{2,1,0:T(8,128)} async-done(((f32[2,128,1024]{2,1,0:T(8,128)}), f32[1,128,1024]{2,1,0:T(8,128)}) %reduce-scatter.6.cloned.1.call-update) | async-done | bytes 524304 | tf_op jit(solution)/shard_map/reduce_scatter | solution.py:16
  93.5 1.8 convert_element_type.9
  95.3 0.0 all-gather.6.cloned.1.call-update
  95.3 1.1 convert_bitcast_fusion
  96.4 1.6 broadcast_in_dim.19
  97.9 4.3 %all-to-all-start = ((bf16[8,128,1024]{2,1,0:T(8,128)(2,1)}), bf16[8,128,1024]{2,1,0:T(8,128)(2,1)S(1)}, u32[]{:S(2)}, u32[]{:S(2)}) async-start(bf16[8,128,1024]{2,1,0:T(8,128)(2,1)} %broadcast_in_dim.19), calls=%async_computation.2 | async-start | bytes 4194304 | tf_op jit(solution)/shard_map/all_to_all | solution.py:33
  102.2 0.0 all-gather.4.cloned.1.call-start
  102.3 88.4 %reduce-scatter.8.cloned.1.call-done = bf16[128,1024]{1,0:T(8,128)(2,1)} async-done(((bf16[1024,1024]{1,0:T(8,128)(2,1)}), bf16[128,1024]{1,0:T(8,128)(2,1)}) %reduce-scatter.8.cloned.1.call-update) | async-done | bytes 262160 | tf_op jit(solution)/shard_map/reduce_scatter | solution.py:59
  190.7 0.0 all-gather.4.cloned.1.call-update
  190.8 37.3 %all-gather.6.cloned.1.call-done = bf16[1,128,16384]{2,1,0:T(8,128)(2,1)} async-done(((bf16[1,128,1024]{2,1,0:T(8,128)(2,1)}), bf16[1,128,16384]{2,1,0:T(8,128)(2,1)}) %all-gather.6.cloned.1.call-update) | async-done | bytes 4194320 | tf_op jit(solution)/shard_map/all_gather | solution.py:90
  228.0 5.0 %copy.7 = bf16[16,8,8,2048]{3,2,1,0:T(8,128)(2,1)S(1)} copy(bf16[16,8,8,2048]{3,1,2,0:T(8,128)(2,1)} %bitcast.25) | data formatting | bytes 8388608
  233.0 4.3 %copy.6 = bf16[128,8,2048]{2,0,1:T(8,128)(2,1)} copy(bf16[128,8,2048]{2,1,0:T(8,128)(2,1)S(1)} %bitcast.24) | data formatting | bytes 8388608 | tf_op jit(solution)/shard_map/all_to_all | solution.py:91
  237.3 0.0 all-to-all-done
  237.3 6.6 %all-to-all-start.1 = ((bf16[128,8,2048]{2,0,1:T(8,128)(2,1)}), bf16[128,8,2048]{2,0,1:T(8,128)(2,1)}, u32[]{:S(2)}, u32[]{:S(2)}) async-start(bf16[128,8,2048]{2,0,1:T(8,128)(2,1)} %copy.6), calls=%async_computation.4 | async-start | bytes 8388608 | tf_op jit(solution)/shard_map/all_to_all | solution.py:91
  245.2 9.0 %fusion.6 = f32[1024,2048]{1,0:T(8,128)} fusion(bf16[1024,1024]{1,0:T(8,128)(2,1)S(1)} %bitcast.27, bf16[1024,2048]{1,0:T(8,128)(2,1)} %param.5), kind=kOutput, calls=%fused_computation.12 | convolution fusion | flops 4294967296 | bytes 14680064 | tf_op jit(solution)/shard_map/dot_general | solution.py:79
  254.2 72.4 %all-gather.4.cloned.1.call-done = bf16[1024,1024]{1,0:T(8,128)(2,1)} async-done(((bf16[128,1024]{1,0:T(8,128)(2,1)}), bf16[1024,1024]{1,0:T(8,128)(2,1)}) %all-gather.4.cloned.1.call-update) | async-done | bytes 2097168 | tf_op jit(solution)/shard_map/all_gather | solution.py:60
  326.6 0.0 all-to-all-done.1
  326.6 18.1 %compare_select_fusion = f32[1024,2048]{1,0:T(8,128)} fusion(f32[1024,2048]{1,0:T(8,128)} %param.4, f32[1024,2048]{1,0:T(8,128)} %fusion.6, f32[]{:T(128)S(6)} %mul.39, f32[]{:T(128)} %bitcast.20, s32[2048]{0:T(1024)S(1)} %iota_add_fusion, s32[1024]{0:T(1024)S(1)} %iota_add_fusion.1, bf16[1024,1024]{1,0:T(8,128)(2,1)} %all-gather.4.cloned.1.call-done, ...), kind=kOutput, calls=%fused_computation | convolution fusion | flops 4326424576 | bytes 31469576 | tf_op jit(solution)/shard_map/dot_general | solution.py:95
  (2 shorter events, 0.0 us)
Async XLA Ops:
  6.5 60.3 %reduce-scatter.4.cloned.1.call-start = ((), (), s32[]{:S(2)}) async-start(), calls=%async_computation.5 | async-start | bytes 5242880 | tf_op jit(solution)/shard_map/reduce_scatter | solution.py:16
  17.3 76.2 %reduce-scatter.6.cloned.1.call-start = ((), (), s32[]{:S(2)}) async-start(), calls=%async_computation.6 | async-start | bytes 1572864 | tf_op jit(solution)/shard_map/reduce_scatter | solution.py:16
  66.8 123.9 %reduce-scatter.8.cloned.1.call-start = ((), (), s32[]{:S(2)}) async-start(), calls=%async_computation.7 | async-start | bytes 2359296 | tf_op jit(solution)/shard_map/reduce_scatter | solution.py:59
  70.4 157.6 %all-gather.6.cloned.1.call-start = ((), (), s32[]{:S(2)}) async-start(), calls=%async_computation.9 | async-start | bytes 4456448 | tf_op jit(solution)/shard_map/all_gather | solution.py:90
  97.9 139.3 %all-to-all-start = ((bf16[8,128,1024]{2,1,0:T(8,128)(2,1)}), bf16[8,128,1024]{2,1,0:T(8,128)(2,1)S(1)}, u32[]{:S(2)}, u32[]{:S(2)}) async-start(bf16[8,128,1024]{2,1,0:T(8,128)(2,1)} %broadcast_in_dim.19), calls=%async_computation.2 | async-start | bytes 4194304 | tf_op jit(solution)/shard_map/all_to_all | solution.py:33
  102.2 224.4 %all-gather.4.cloned.1.call-start = ((), (), s32[]{:S(2)}) async-start(), calls=%async_computation.8 | async-start | bytes 2359296 | tf_op jit(solution)/shard_map/all_gather | solution.py:60
  237.3 89.4 %all-to-all-start.1 = ((bf16[128,8,2048]{2,0,1:T(8,128)(2,1)}), bf16[128,8,2048]{2,0,1:T(8,128)(2,1)}, u32[]{:S(2)}, u32[]{:S(2)}) async-start(bf16[128,8,2048]{2,0,1:T(8,128)(2,1)} %copy.6), calls=%async_computation.4 | async-start | bytes 8388608 | tf_op jit(solution)/shard_map/all_to_all | solution.py:91
Sparse Core Ops, SparseCore 0:
  17.4 49.3 reduce-scatter.3
  69.2 24.2 reduce-scatter.5
  97.3 93.4 reduce-scatter.7
  192.2 35.7 all-gather.5
  230.2 96.3 all-gather.3
where the time goes:
time: 352 us; the launch traced here: 351 us
  waiting for transfers between devices  271 us (77%)
  matrix products  35.3 us (10%)
  between operations  14.5 us (4%)
  local copies, waits for them, and re-layouts  13.4 us (4%)
  starting transfers between devices  11 us (3%)
  other arithmetic  6.3 us (2%)
    reduce_scatter x1, waiting for transfers between devices, spread(): own = lax.psum_scatter(padded, axis, scatter_dimension=0, tiled=True)  88.4 us
    reduce_scatter x2, waiting for transfers between devices, reduced_to_own(): pieces = lax.psum_scatter(pieces, axes[k], scatter_dimension=0, tiled=True)  72.5 us
    all_gather x1, waiting for transfers between devices, spread(): lax.all_gather(own, axis, axis=0, tiled=True)[:len(lines)]  72.4 us
    all_gather x1, waiting for transfers between devices, per_device(): full_panel = lax.all_gather(projected, 'row', axis=1, tiled=True)  37.3 us
    dot_general x1, matrix products, per_device(): lax.dot_general(own_columns, dealt, (((0,), (0,)), ((), ())), preferred_e...  18.1 us
    dot_general x1, matrix products, per_device(): lax.dot_general(gather_directly(projected, COL, 0), sample_part, (((0,),...  9.04 us
    dot_general x1, matrix products, per_device(): lax.dot_general(sample_part, rounded, (((1,), (1,)), ((), ())), preferred...  8.22 us
  transfers between devices with their start and end apart: 7, of which 5 were waited for; matrix products, arithmetic and copies ran while one was open for 7% of the time, Pallas kernels for 0%

commit v1 on v0

v1 whole, which is shorter than its diff:
```python
import functools
import itertools

import jax
import jax.numpy as jnp
from jax import lax
from jax.experimental import pallas as pl
from jax.experimental.pallas import tpu as pltpu
from jax.sharding import Mesh
from jax.sharding import PartitionSpec as P


SIZES = (4, 2, 2, 2, 4)
NAMES = ("x", "zl", "core", "zh", "y")
ROW = ("x", "zl", "core")
COL = ("zh", "y")


def number(x, zl, h, zh, y):
    return (((x * 2 + zl) * 2 + h) * 2 + zh) * 4 + y


def places():
    return itertools.product(*(range(n) for n in SIZES))


def crossing_of_sums():
    return [
        (number(x, zl, h, zh, y), number(y, zh, h, x // 2, x % 2 * 2 + zl))
        for x, zl, h, zh, y in places()
    ]


def crossing_of_samples():
    return [
        (number(x, zl, h, zh, y), number(zh * 2 + y // 2, y % 2, h, zl, x))
        for x, zl, h, zh, y in places()
    ]


def sent_to_all(array, axes, length):
    copies = jnp.broadcast_to(array[None], (length, *array.shape))
    return lax.all_to_all(copies, axes, 0, 0, tiled=True)


TILE = 256


def update_kernel(samples_count, whole, scalars, yr, xr, xc, mine, other, precision, out):
    width = mine.shape[1]
    m, t = pl.program_id(0), pl.program_id(1)
    side = (whole[0] + t) % 2
    rows = pl.ds(pl.multiple_of(m * TILE, TILE), TILE)
    contract = (((0,), (0,)), ((), ()))

    def finish(panel):
        total = lax.dot_general(
            yr[:, rows],
            xc[:, pl.ds(pl.multiple_of(side * width, width), width)],
            contract,
            preferred_element_type=jnp.float32,
        )
        total = total + lax.dot_general(
            xr[:, rows], panel[...], contract, preferred_element_type=jnp.float32
        )
        gradient = total * (1.0 / samples_count)
        step, level = scalars[0], scalars[1]
        first_row = whole[1] + m * TILE
        first_col = whole[2] + side * width
        stepped = precision[...] - step * gradient
        out[...] = stepped - jnp.clip(stepped, -level, level)

        @pl.when((first_row < first_col + width) & (first_col < first_row + TILE))
        def _():
            row = first_row + lax.broadcasted_iota(jnp.int32, stepped.shape, 0)
            col = first_col + lax.broadcasted_iota(jnp.int32, stepped.shape, 1)
            own = precision[...]
            on_diagonal = row == col
            lowered = own - step * (gradient - 1.0 / jnp.where(on_diagonal, own, 1.0))
            out[...] = jnp.where(on_diagonal, lowered, out[...])

    @pl.when(t == 0)
    def _():
        finish(mine)

    @pl.when(t == 1)
    def _():
        finish(other)


def updated_tile(whole, scalars, yr, xr, xc, mine, other, precision):
    rows, cols = precision.shape
    width = mine.shape[1]
    inside = pl.BlockSpec(memory_space=pltpu.VMEM)
    tile = pl.BlockSpec((TILE, width), lambda m, t, whole: (m, (whole[0] + t) % 2))
    depth = 2 * xc.shape[0]
    return pl.pallas_call(
        functools.partial(update_kernel, xc.shape[0]),
        out_shape=jax.ShapeDtypeStruct(precision.shape, precision.dtype),
        grid_spec=pltpu.PrefetchScalarGridSpec(
            num_scalar_prefetch=1,
            grid=(rows // TILE, cols // width),
            in_specs=[pl.BlockSpec(memory_space=pltpu.SMEM)] + [inside] * 5 + [tile],
            out_specs=tile,
        ),
        compiler_params=pltpu.CompilerParams(vmem_limit_bytes=48 << 20),
        cost_estimate=pl.CostEstimate(
            flops=2 * rows * cols * depth, bytes_accessed=28 << 20, transcendentals=0
        ),
        name="update",
    )(whole, scalars, yr, xr, xc, mine, other, precision)


def per_device(precision, samples, step_size, threshold):
    rows_tile, cols_tile = precision.shape
    sample_count = samples.shape[0]
    x, zl, h, zh, y = (lax.axis_index(a) for a in NAMES)
    parts = 8
    piece = sample_count // parts

    mine = lax.dynamic_slice(
        samples, (x * 2 * piece, h * rows_tile), (2 * piece, rows_tile)
    )
    own_quarter = lax.ppermute(mine, NAMES, crossing_of_samples())
    rounded = precision.astype(jnp.bfloat16)
    partial = lax.dot_general(
        samples, rounded, (((1,), (1,)), ((), ())), preferred_element_type=jnp.float32
    ).astype(jnp.bfloat16)
    shares = lax.all_to_all(
        partial.reshape(parts, piece, rows_tile), ("y", "zh"), 0, 0, tiled=True
    )
    own_quarter = own_quarter * jnp.bfloat16(0.5)
    own_columns = lax.all_gather(own_quarter, "y", axis=0, tiled=True)
    total = jnp.sum(shares.astype(jnp.float32), axis=0)
    projected = total.astype(jnp.bfloat16)
    halved = projected * jnp.bfloat16(0.5)

    crossed = lax.ppermute(projected, NAMES, crossing_of_sums())
    pair = lax.all_gather(halved, "zh", axis=0, tiled=True)
    crossed, pair = lax.optimization_barrier((crossed, pair))
    pair, own_columns = lax.optimization_barrier((pair, own_columns))
    row_panel = lax.all_gather(pair, "y", axis=0, tiled=True)
    panel = sent_to_all(crossed, ("x", "zl"), parts).reshape(sample_count, rows_tile)
    other_panel = lax.ppermute(panel, "core", [(0, 1), (1, 0)])

    row_start = ((x * 2 + zl) * 2 + h) * rows_tile
    col_start = (zh * 4 + y) * cols_tile
    whole = jnp.stack([h, row_start, col_start]).astype(jnp.int32)
    scalars = jnp.stack([step_size[0], step_size[0] * threshold[0]])
    return updated_tile(
        whole, scalars, row_panel, own_columns, samples, panel, other_panel, precision
    )


def solution(mesh):
    split = Mesh(mesh.devices.reshape(SIZES), NAMES)
    placed = (P(ROW, COL), P(None, COL), P(), P())
    return jax.shard_map(
        per_device, mesh=split, in_specs=placed, out_specs=P(ROW, COL), check_vma=False
    )
```

time: 352 us -> 188 us (0.53)
  waiting for transfers between devices: 271 us -> 33.8 us
  blocking collectives: 0 us -> 95.6 us
  matrix products: 35.3 us -> 9.18 us
  Pallas kernels: 0 us -> 18.5 us
  local copies, waits for them, and re-layouts: 13.4 us -> 5.85 us
  other arithmetic: 6.3 us -> 1.38 us
  starting transfers between devices: 11 us -> 7.34 us
    reduce_scatter x3 -> x0, waiting for transfers between devices: 161 us -> none  [the longest x1 88.4 us: spread(): own = lax.psum_scatter(padded, axis, scatter_dimension=0, tiled=True)]
    all_gather x2, waiting for transfers between devices: 110 us -> 0.02 us  [the longest x1 0.02 us: per_device(): own_columns = lax.all_gather(own_quarter, 'y', axis=0, tiled=True)]
    all_to_all x0 -> x1, blocking collectives: none -> 79.3 us  [per_device(): lax.all_to_all(partial.reshape(parts, piece, rows_tile), ('y', 'zh'), 0,...]
    all_to_all x2 -> x1, waiting for transfers between devices: 0.01 us -> 30.3 us  [sent_to_all(): return lax.all_to_all(copies, axes, 0, 0, tiled=True)]
    dot_general x3 -> x1, matrix products: 35.3 us -> 9.18 us  [per_device(): lax.dot_general(samples, rounded, (((1,), (1,)), ((), ())), preferred_ele...]
    pallas_call x0 -> x1, Pallas kernels: none -> 18.5 us  [updated_tile(): pl.pallas_call(functools.partial(update_kernel, xc.shape[0]), out_shape=j...]
    all_gather x0 -> x1, blocking collectives: none -> 16.3 us  [per_device(): pair = lax.all_gather(halved, 'zh', axis=0, tiled=True)]
    all_to_all x2 -> x1, starting transfers between devices: 10.9 us -> 5.92 us  [sent_to_all(): return lax.all_to_all(copies, axes, 0, 0, tiled=True)]
  transfers between devices with their start and end apart: 7 -> 6, of which waited for: 5 -> 2; matrix products, arithmetic and copies ran while one was open for 7% -> 6% of each run, Pallas kernels for 0% -> 0%
where the time goes in v1:
time: 188 us; the launch traced here: 186 us
  blocking collectives  95.6 us (51%)
  waiting for transfers between devices  33.8 us (18%)
  Pallas kernels  18.5 us (10%)
  between operations  14.8 us (8%)
  matrix products  9.18 us (5%)
  starting transfers between devices  7.34 us (4%)
  local copies, waits for them, and re-layouts  5.85 us (3%)
    all_to_all x1, blocking collectives, per_device(): lax.all_to_all(partial.reshape(parts, piece, rows_tile), ('y', 'zh'), 0,...  79.3 us
    all_to_all x1, waiting for transfers between devices, sent_to_all(): return lax.all_to_all(copies, axes, 0, 0, tiled=True)  30.3 us
    pallas_call x1, Pallas kernels, updated_tile(): pl.pallas_call(functools.partial(update_kernel, xc.shape[0]), out_shape=j...  18.5 us
    all_gather x1, blocking collectives, per_device(): pair = lax.all_gather(halved, 'zh', axis=0, tiled=True)  16.3 us
    dot_general x1, matrix products, per_device(): lax.dot_general(samples, rounded, (((1,), (1,)), ((), ())), preferred_ele...  9.18 us
    all_to_all x1, starting transfers between devices, sent_to_all(): return lax.all_to_all(copies, axes, 0, 0, tiled=True)  5.92 us
  transfers between devices with their start and end apart: 6, of which 2 were waited for; matrix products, arithmetic and copies ran while one was open for 6% of the time, Pallas kernels for 0%

profile of v1, /device:TPU:0, one launch (start us, length us, event | category | flops | bytes accessed | tf_op | source)
XLA Modules:
  0.0 186.4 jit_solution(14540960260806398663)
XLA Ops:
  6.5 0.0 all-gather.3.cloned.1.call-start
  6.5 1.1 dynamic_slice.3
  7.6 0.7 collective-permute-start.1
  8.3 0.0 collective-permute-done.1
  8.3 0.8 broadcast_multiply_fusion
  9.2 0.0 all-gather.3.cloned.1.call-update
  9.2 9.2 %fusion.2 = bf16[1024,1024]{1,0:T(8,128)(2,1)S(1)} fusion(bf16[1024,2048]{1,0:T(8,128)(2,1)} %xc.1, f32[1024,2048]{1,0:T(8,128)} %precision.1), kind=kOutput, calls=%fused_computation.2 | convolution fusion | flops 4298113024 | bytes 14680064 | tf_op jit(solution)/shard_map/dot_general | solution.py:126
  18.4 79.3 %all_to_all.10 = bf16[8,128,1024]{2,1,0:T(8,128)(2,1)S(1)} all-to-all(bf16[8,128,1024]{2,1,0:T(8,128)(2,1)S(1)} %bitcast.8), channel_id=1, replica_groups=mesh['x'=4,'zl'=2,'core'=2,'zh'=2,'y'=4] {'y','zh'}, dimensions={0} | all-to-all | bytes 4194304 | tf_op jit(solution)/shard_map/all_to_all | solution.py:129
  97.7 0.4 reduce_sum.12
  98.0 0.7 collective-permute-start
  98.8 16.3 %all_gather.9 = bf16[256,1024]{1,0:T(8,128)(2,1)} all-gather(bf16[128,1024]{1,0:T(8,128)(2,1)S(1)} %broadcast_multiply_fusion.1), channel_id=1, replica_groups=mesh['x'=4,'zl'=2,'core'=2,'zh'=2,'y'=4] {'zh'}, dimensions={0}, use_global_device_ids=true | all-gather | bytes 786432 | tf_op jit(solution)/shard_map/all_gather | solution.py:139
  115.1 0.0 collective-permute-done
  115.1 1.6 broadcast_in_dim.2
  116.6 5.9 %all-to-all-start.1 = ((bf16[8,128,1024]{2,1,0:T(8,128)(2,1)}), bf16[8,128,1024]{2,1,0:T(8,128)(2,1)S(1)}, u32[]{:S(2)}, u32[]{:S(2)}) async-start(bf16[8,128,1024]{2,1,0:T(8,128)(2,1)} %broadcast_in_dim.2), calls=%async_computation.1 | async-start | bytes 4194304 | tf_op jit(solution)/shard_map/all_to_all | solution.py:43
  122.6 0.0 all-gather.5.cloned.1.call-start
  122.6 0.0 all-gather.3.cloned.1.call-done.xr
  122.6 0.7 all-gather.5.cloned.1.call-update
  123.3 30.3 %all-to-all-done.1 = bf16[8,128,1024]{2,1,0:T(8,128)(2,1)S(1)} async-done(((bf16[8,128,1024]{2,1,0:T(8,128)(2,1)}), bf16[8,128,1024]{2,1,0:T(8,128)(2,1)S(1)}, u32[]{:S(2)}, u32[]{:S(2)}) %all-to-all-start.1) | async-done | bytes 2097184 | tf_op jit(solution)/shard_map/all_to_all | solution.py:43
  153.6 0.0 copy-start.2
  153.6 0.0 collective-permute-start.2
  154.9 0.1 pad_maximum_fusion.scalars
  155.0 0.1 pad_add_fusion.whole
  155.1 2.8 %collective-permute-done.2.other = bf16[1024,1024]{1,0:T(8,128)(2,1)} collective-permute-done((bf16[1024,1024]{1,0:T(8,128)(2,1)S(1)}, bf16[1024,1024]{1,0:T(8,128)(2,1)}, u32[]{:S(2)}, u32[]{:S(2)}) %collective-permute-start.2) | collective-permute-done | bytes 2097184 | tf_op jit(solution)/shard_map/ppermute | solution.py:144
  157.9 0.0 all-gather.5.cloned.1.call-done.yr
  157.9 0.0 copy-done.2
  157.9 0.0 copy-start
  157.9 1.6 copy-done
  159.5 0.0 copy-start.1
  159.5 1.6 copy-done.1
  161.1 18.5 %update.1 = f32[1024,2048]{1,0:T(8,128)} custom-call(s32[3]{0:T(128)S(1)} %pad_add_fusion.whole, f32[2]{0:T(128)S(1)} %pad_maximum_fusion.scalars, bf16[1024,1024]{1,0:T(8,128)(2,1)S(1)} %copy-done.1, bf16[1024,1024]{1,0:T(8,128)(2,1)S(1)} %copy-done, bf16[1024,2048]{1,0:T(8,128)(2,1)} %xc.1, bf16[1024,1024]{1,0:T(8,128)(2,1)} %bitcast.7, ...), custom_call_target="tpu_custom_call" | custom-call | flops 8589934592 | bytes 29360128 | tf_op jit(solution)/shard_map/update/pallas_call | solution.py:97
  (1 shorter events, 0.0 us)
Async XLA Ops:
  6.5 116.1 %all-gather.3.cloned.1.call-start = ((), (), s32[]{:S(2)}) async-start(), calls=%async_computation.2 | async-start | bytes 2621440 | tf_op jit(solution)/shard_map/all_gather | solution.py:133
  7.6 0.7 collective-permute-start.1
  98.0 17.0 %collective-permute-start = (bf16[128,1024]{1,0:T(8,128)(2,1)S(1)}, bf16[128,1024]{1,0:T(8,128)(2,1)S(1)}, u32[]{:S(2)}, u32[]{:S(2)}) collective-permute-start(bf16[128,1024]{1,0:T(8,128)(2,1)S(1)} %reduce_sum.12), channel_id=1, source_target_pairs={{0,0},{1,32},{2,64},{3,96},{4,16},{5,48},{6,80},{7,112},{8,8},{9,4... | collective-permute-start | bytes 786440 | tf_op jit(solution)/shard_map/ppermute | solution.py:138
  116.6 37.0 %all-to-all-start.1 = ((bf16[8,128,1024]{2,1,0:T(8,128)(2,1)}), bf16[8,128,1024]{2,1,0:T(8,128)(2,1)S(1)}, u32[]{:S(2)}, u32[]{:S(2)}) async-start(bf16[8,128,1024]{2,1,0:T(8,128)(2,1)} %broadcast_in_dim.2), calls=%async_computation.1 | async-start | bytes 4194304 | tf_op jit(solution)/shard_map/all_to_all | solution.py:43
  122.6 35.3 %all-gather.5.cloned.1.call-start = ((), (), s32[]{:S(2)}) async-start(), calls=%async_computation.3 | async-start | bytes 2621440 | tf_op jit(solution)/shard_map/all_gather | solution.py:142
  153.6 4.3 %copy-start.2 = (bf16[8,128,1024]{2,1,0:T(8,128)(2,1)}, bf16[8,128,1024]{2,1,0:T(8,128)(2,1)S(1)}, u32[]{:S(2)}) copy-start(bf16[8,128,1024]{2,1,0:T(8,128)(2,1)S(1)} %all-to-all-done.1) | copy-start | bytes 6291460
  153.6 4.3 %collective-permute-start.2 = (bf16[1024,1024]{1,0:T(8,128)(2,1)S(1)}, bf16[1024,1024]{1,0:T(8,128)(2,1)}, u32[]{:S(2)}, u32[]{:S(2)}) collective-permute-start(bf16[1024,1024]{1,0:T(8,128)(2,1)S(1)} %bitcast.6), channel_id=1, source_target_pairs={{0,8},{8,0},{1,9},{9,1},{2,10},{10,2},{3,11},{11,3},{4,12},{12,4},... | collective-permute-start | bytes 6291464 | tf_op jit(solution)/shard_map/ppermute | solution.py:144
  157.9 1.6 copy-start
  159.5 1.6 copy-start.1
Sparse Core Ops, SparseCore 0:
  9.3 86.1 all-gather.2
  125.0 30.9 all-gather.4

commit v2 on v1

v2 whole, which is shorter than its diff:
```python
import functools
import itertools

import jax
import jax.numpy as jnp
from jax import lax
from jax.experimental import pallas as pl
from jax.experimental.pallas import tpu as pltpu
from jax.sharding import Mesh
from jax.sharding import PartitionSpec as P


SIZES = (4, 2, 2, 2, 4)
NAMES = ("x", "zl", "core", "zh", "y")
ROW = ("x", "zl", "core")
COL = ("zh", "y")


def number(x, zl, h, zh, y):
    return (((x * 2 + zl) * 2 + h) * 2 + zh) * 4 + y


def places():
    return itertools.product(*(range(n) for n in SIZES))


def crossing_of_sums():
    return [
        (number(x, zl, h, zh, y), number(y, zh, h, x // 2, x % 2 * 2 + zl))
        for x, zl, h, zh, y in places()
    ]


def crossing_of_samples():
    return [
        (number(x, zl, h, zh, y), number(zh * 2 + y // 2, y % 2, h, zl ^ zh, (x + y) % 4))
        for x, zl, h, zh, y in places()
    ]


def sent_to_all(array, axes, length):
    copies = jnp.broadcast_to(array[None], (length, *array.shape))
    return lax.all_to_all(copies, axes, 0, 0, tiled=True)


TILE = 256
STRIP = 512


def partial_kernel(samples, precision, out):
    out[...] = lax.dot_general(
        samples[...],
        precision[...].astype(jnp.bfloat16),
        (((1,), (1,)), ((), ())),
        preferred_element_type=jnp.float32,
    ).astype(jnp.bfloat16)


def partial_sums(samples, precision):
    count, width = samples.shape
    rows = precision.shape[0]
    return pl.pallas_call(
        partial_kernel,
        out_shape=jax.ShapeDtypeStruct((count, rows), jnp.bfloat16),
        grid=(rows // STRIP,),
        in_specs=[
            pl.BlockSpec((count, width), lambda r: (0, 0)),
            pl.BlockSpec((STRIP, width), lambda r: (r, 0)),
        ],
        out_specs=pl.BlockSpec((count, STRIP), lambda r: (0, r)),
        compiler_params=pltpu.CompilerParams(vmem_limit_bytes=40 << 20),
        cost_estimate=pl.CostEstimate(
            flops=2 * count * rows * width, bytes_accessed=14 << 20, transcendentals=0
        ),
        name="partial",
    )(samples, precision)


def update_kernel(
    samples_count, whole, scalars, yr, x0, x1, x2, x3, xc, mine, other, precision, out, kept
):
    deep = x0.shape[0]
    t = pl.program_id(0)
    per_side = pl.num_programs(0) // 2
    contract = (((0,), (0,)), ((), ()))
    step, level = scalars[0], scalars[1]

    def finish(panel):
        total = lax.dot_general(yr[...], xc[...], contract, preferred_element_type=jnp.float32)
        for d, quarter in enumerate((x0, x1, x2, x3)):
            start = pl.multiple_of(whole[3 + d] * deep, deep)
            total = total + lax.dot_general(
                quarter[...],
                panel[pl.ds(start, deep), :],
                contract,
                preferred_element_type=jnp.float32,
            )
        gradient = total * (1.0 / samples_count)
        stepped = precision[...] - step * gradient
        out[...] = stepped - jnp.clip(stepped, -level, level)
        side = (whole[0] + t // per_side) % 2
        offset = whole[2] + (side * per_side + t % per_side) * TILE - whole[1]

        @pl.when((offset >= 0) & (offset < out.shape[0]))
        def _():
            kept[...] = stepped
            rows = pl.ds(pl.multiple_of(offset, TILE), TILE)
            own, shrunk = precision[rows, :], out[rows, :]
            on_diagonal = lax.broadcasted_iota(jnp.int32, own.shape, 0) == (
                lax.broadcasted_iota(jnp.int32, own.shape, 1)
            )
            raised = kept[rows, :] + step / jnp.where(on_diagonal, own, 1.0)
            out[rows, :] = jnp.where(on_diagonal, raised, shrunk)

    @pl.when(t < per_side)
    def _():
        finish(mine)

    @pl.when(t >= per_side)
    def _():
        finish(other)


def updated_tile(whole, scalars, yr, quarters, xc, mine, other, precision):
    rows, cols = precision.shape
    count = xc.shape[0]
    per_side = cols // TILE // 2
    inside = pl.BlockSpec(memory_space=pltpu.VMEM)

    def column(t, whole):
        return 0, (whole[0] + t // per_side) % 2 * per_side + t % per_side

    tile = pl.BlockSpec((rows, TILE), column)
    yr = pltpu.with_memory_space_constraint(yr, pltpu.HBM)
    return pl.pallas_call(
        functools.partial(update_kernel, count),
        out_shape=jax.ShapeDtypeStruct(precision.shape, precision.dtype),
        grid_spec=pltpu.PrefetchScalarGridSpec(
            num_scalar_prefetch=1,
            grid=(2 * per_side,),
            in_specs=[
                pl.BlockSpec(memory_space=pltpu.SMEM),
                pl.BlockSpec(yr.shape, lambda t, whole: (0, 0)),
                inside,
                inside,
                inside,
                inside,
                pl.BlockSpec((count, TILE), column),
                pl.BlockSpec((count, TILE), lambda t, whole: (0, jnp.minimum(t, per_side - 1))),
                pl.BlockSpec((count, TILE), lambda t, whole: (0, jnp.maximum(t - per_side, 0))),
                tile,
            ],
            out_specs=tile,
            scratch_shapes=[pltpu.VMEM((rows, TILE), jnp.float32)],
        ),
        compiler_params=pltpu.CompilerParams(vmem_limit_bytes=48 << 20),
        cost_estimate=pl.CostEstimate(
            flops=4 * rows * cols * count, bytes_accessed=28 << 20, transcendentals=0
        ),
        name="update",
    )(whole, scalars, yr, *quarters, xc, mine, other, precision)


def per_device(precision, samples, step_size, threshold):
    rows_tile, cols_tile = precision.shape
    sample_count = samples.shape[0]
    x, zl, h, zh, y = (lax.axis_index(a) for a in NAMES)
    parts = 8
    piece = sample_count // parts

    mine = lax.dynamic_slice(
        samples, ((x + y) % 4 * 2 * piece, h * rows_tile), (2 * piece, rows_tile)
    )
    own_quarter = lax.ppermute(mine, NAMES, crossing_of_samples())
    partial = partial_sums(samples, precision)
    shares = lax.all_to_all(partial.reshape(parts, piece, rows_tile), ("y", "zh"), 0, 0, tiled=True)
    own_quarter = own_quarter * jnp.bfloat16(0.5)
    total = jnp.sum(shares.astype(jnp.float32), axis=0)
    projected = total.astype(jnp.bfloat16)
    halved = projected * jnp.bfloat16(0.5)

    crossed = lax.ppermute(projected, NAMES, crossing_of_sums())
    pair = lax.all_gather(halved, "zh", axis=0, tiled=True)
    crossed, pair = lax.optimization_barrier((crossed, pair))
    own_quarter, pair = lax.optimization_barrier((own_quarter, pair))
    row_panel = lax.all_gather(pair, "y", axis=0, tiled=True)
    quarters = [own_quarter]
    for turn in (1, 3, 2):
        moves = [(i, (i + turn) % 4) for i in range(4)]
        quarters.append(lax.ppermute(own_quarter, "y", moves))
    panel = sent_to_all(crossed, ("x", "zl"), parts).reshape(sample_count, rows_tile)
    other_panel = lax.ppermute(panel, "core", [(0, 1), (1, 0)])

    row_start = ((x * 2 + zl) * 2 + h) * rows_tile
    col_start = (zh * 4 + y) * cols_tile
    places_of = [(y - turn) % 4 for turn in (0, 1, 3, 2)]
    whole = jnp.stack([h, row_start, col_start, *places_of]).astype(jnp.int32)
    scalars = jnp.stack([step_size[0], step_size[0] * threshold[0]])
    return updated_tile(
        whole, scalars, row_panel, quarters, samples, panel, other_panel, precision
    )


def solution(mesh):
    split = Mesh(mesh.devices.reshape(SIZES), NAMES)
    placed = (P(ROW, COL), P(None, COL), P(), P())
    return jax.shard_map(
        per_device, mesh=split, in_specs=placed, out_specs=P(ROW, COL), check_vma=False
    )
```

time: 188 us -> 203 us (1.080)
  the two profiles are of different devices: /device:TPU:0 before, /device:TPU:97 now
where the time goes in v2:
time: 203 us; the launch traced here: 202 us
  waiting for transfers between devices  94.7 us (47%)
  blocking collectives  39.9 us (20%)
  Pallas kernels  24.1 us (12%)
  starting transfers between devices  21.7 us (11%)
  between operations  14.8 us (7%)
  local copies, waits for them, and re-layouts  4.93 us (2%)
  other arithmetic  2.11 us (1%)
    ppermute x1, waiting for transfers between devices, per_device(): own_quarter = lax.ppermute(mine, NAMES, crossing_of_samples())  51.7 us
    ppermute x3, waiting for transfers between devices, per_device(): quarters.append(lax.ppermute(own_quarter, 'y', moves))  34.8 us
    all_to_all x1, blocking collectives, per_device(): lax.all_to_all(partial.reshape(parts, piece, rows_tile), ('y', 'zh'), 0,...  32.2 us
    pallas_call x1, Pallas kernels, updated_tile(): pl.pallas_call(functools.partial(update_kernel, count), out_shape=jax.Sha...  17 us
    all_to_all x1, starting transfers between devices, sent_to_all(): return lax.all_to_all(copies, axes, 0, 0, tiled=True)  10.9 us
    all_gather x1, blocking collectives, per_device(): pair = lax.all_gather(halved, 'zh', axis=0, tiled=True)  7.69 us
    pallas_call x1, Pallas kernels, partial_sums(): pl.pallas_call(partial_kernel, out_shape=jax.ShapeDtypeStruct((count, row...  7.08 us
    all_gather x1, waiting for transfers between devices, per_device(): row_panel = lax.all_gather(pair, 'y', axis=0, tiled=True)  6.03 us
  transfers between devices with their start and end apart: 8, of which 6 were waited for; matrix products, arithmetic and copies ran while one was open for 1% of the time, Pallas kernels for 0%

profile of v2, /device:TPU:97, one launch (start us, length us, event | category | flops | bytes accessed | tf_op | source)
XLA Modules:
  0.0 202.2 jit_solution(13462794405295006058)
XLA Ops:
  6.5 0.0 copy-start
  6.5 2.2 %copy-done = bf16[1024,2048]{1,0:T(8,128)(2,1)S(1)} copy-done((bf16[1024,2048]{1,0:T(8,128)(2,1)S(1)}, bf16[1024,2048]{1,0:T(8,128)(2,1)}, u32[]{:S(2)}) %copy-start) | copy-done | bytes 4194328
  8.7 7.1 %partial.1 = bf16[1024,1024]{1,0:T(8,128)(2,1)S(1)} custom-call(bf16[1024,2048]{1,0:T(8,128)(2,1)S(1)} %copy-done, f32[1024,2048]{1,0:T(8,128)} %precision.3), custom_call_target="tpu_custom_call" | custom-call | flops 4294967296 | bytes 14680064 | tf_op jit(solution)/shard_map/partial/pallas_call | solution.py:62
  15.8 32.2 %all_to_all.10 = bf16[8,128,1024]{2,1,0:T(8,128)(2,1)} all-to-all(bf16[8,128,1024]{2,1,0:T(8,128)(2,1)S(1)} %bitcast.11), channel_id=1, replica_groups=mesh['x'=4,'zl'=2,'core'=2,'zh'=2,'y'=4] {'y','zh'}, dimensions={0} | all-to-all | bytes 4194304 | tf_op jit(solution)/shard_map/all_to_all | solution.py:176
  48.0 2.0 reduce_sum.12
  50.0 2.9 %collective-permute-start.1 = (bf16[128,1024]{1,0:T(8,128)(2,1)S(1)}, bf16[128,1024]{1,0:T(8,128)(2,1)S(1)}, u32[]{:S(2)}, u32[]{:S(2)}) collective-permute-start(bf16[128,1024]{1,0:T(8,128)(2,1)S(1)} %reduce_sum.12), channel_id=1, source_target_pairs={{0,0},{1,32},{2,64},{3,96},{4,16},{5,48},{6,80},{7,112},{8,8},{9,4... | collective-permute-start | bytes 786440 | tf_op jit(solution)/shard_map/ppermute | solution.py:182
  52.9 7.7 %all_gather.6 = bf16[256,1024]{1,0:T(8,128)(2,1)} all-gather(bf16[128,1024]{1,0:T(8,128)(2,1)S(1)} %broadcast_multiply_fusion.1), channel_id=1, replica_groups=mesh['x'=4,'zl'=2,'core'=2,'zh'=2,'y'=4] {'zh'}, dimensions={0}, use_global_device_ids=true | all-gather | bytes 786432 | tf_op jit(solution)/shard_map/all_gather | solution.py:183
  60.6 2.1 %collective-permute-done.1 = bf16[128,1024]{1,0:T(8,128)(2,1)S(1)} collective-permute-done((bf16[128,1024]{1,0:T(8,128)(2,1)S(1)}, bf16[128,1024]{1,0:T(8,128)(2,1)S(1)}, u32[]{:S(2)}, u32[]{:S(2)}) %collective-permute-start.1) | collective-permute-done | bytes 262176 | tf_op jit(solution)/shard_map/ppermute | solution.py:182
  62.8 1.6 broadcast_in_dim.2
  64.4 10.9 %all-to-all-start.1 = ((bf16[8,128,1024]{2,1,0:T(8,128)(2,1)}), bf16[8,128,1024]{2,1,0:T(8,128)(2,1)S(1)}, u32[]{:S(2)}, u32[]{:S(2)}) async-start(bf16[8,128,1024]{2,1,0:T(8,128)(2,1)} %broadcast_in_dim.2), calls=%async_computation.1 | async-start | bytes 4194304 | tf_op jit(solution)/shard_map/all_to_all | solution.py:43
  75.3 0.0 all-gather.2.cloned.1.call-start
  75.3 1.1 dynamic_slice.3
  76.4 5.4 %collective-permute-start = (bf16[256,1024]{1,0:T(8,128)(2,1)S(1)}, bf16[256,1024]{1,0:T(8,128)(2,1)S(1)}, u32[]{:S(2)}, u32[]{:S(2)}) collective-permute-start(bf16[256,1024]{1,0:T(8,128)(2,1)S(1)} %dynamic_slice.3), channel_id=1, source_target_pairs={{0,0},{1,17},{2,34},{3,51},{4,68},{5,85},{6,102},{7,119},{8,8},{9,... | collective-permute-start | bytes 1572872 | tf_op jit(solution)/shard_map/ppermute | solution.py:174
  81.8 51.7 %collective-permute-done = bf16[256,1024]{1,0:T(8,128)(2,1)S(1)} collective-permute-done((bf16[256,1024]{1,0:T(8,128)(2,1)S(1)}, bf16[256,1024]{1,0:T(8,128)(2,1)S(1)}, u32[]{:S(2)}, u32[]{:S(2)}) %collective-permute-start) | collective-permute-done | bytes 524320 | tf_op jit(solution)/shard_map/ppermute | solution.py:174
  133.5 0.0 all-gather.2.cloned.1.call-update
  133.6 0.0 all-to-all-done.1
  133.6 1.0 collective-permute-start.5
  134.5 0.0 collective-permute-start.4
  134.5 0.0 collective-permute-start.3
  134.5 1.5 collective-permute-start.2
  137.3 0.1 stack.35.whole
  137.4 0.1 pad_maximum_fusion.scalars
  137.5 17.2 %collective-permute-done.4.x3 = bf16[256,1024]{1,0:T(8,128)(2,1)S(1)} collective-permute-done((bf16[256,1024]{1,0:T(8,128)(2,1)S(1)}, bf16[256,1024]{1,0:T(8,128)(2,1)S(1)}, u32[]{:S(2)}, u32[]{:S(2)}) %collective-permute-start.4) | collective-permute-done | bytes 524320 | tf_op jit(solution)/shard_map/ppermute | solution.py:190
  154.6 6.3 %collective-permute-done.3.x2 = bf16[256,1024]{1,0:T(8,128)(2,1)} collective-permute-done((bf16[256,1024]{1,0:T(8,128)(2,1)S(1)}, bf16[256,1024]{1,0:T(8,128)(2,1)}, u32[]{:S(2)}, u32[]{:S(2)}) %collective-permute-start.3) | collective-permute-done | bytes 524320 | tf_op jit(solution)/shard_map/ppermute | solution.py:190
  161.0 11.3 %collective-permute-done.2.x1 = bf16[256,1024]{1,0:T(8,128)(2,1)} collective-permute-done((bf16[256,1024]{1,0:T(8,128)(2,1)S(1)}, bf16[256,1024]{1,0:T(8,128)(2,1)}, u32[]{:S(2)}, u32[]{:S(2)}) %collective-permute-start.2) | collective-permute-done | bytes 524320 | tf_op jit(solution)/shard_map/ppermute | solution.py:190
  172.3 6.0 %all-gather.2.cloned.1.call-done.yr = bf16[1024,1024]{1,0:T(8,128)(2,1)} async-done(((bf16[256,1024]{1,0:T(8,128)(2,1)}), bf16[1024,1024]{1,0:T(8,128)(2,1)}) %all-gather.2.cloned.1.call-update) | async-done | bytes 2097168 | tf_op jit(solution)/shard_map/all_gather | solution.py:186
  178.3 0.0 collective-permute-done.5.other
  178.3 17.0 %update.1 = f32[1024,2048]{1,0:T(8,128)} custom-call(s32[7]{0:T(128)S(1)} %stack.35.whole, f32[2]{0:T(128)S(1)} %pad_maximum_fusion.scalars, bf16[1024,1024]{1,0:T(8,128)(2,1)} %all-gather.2.cloned.1.call-done.yr, bf16[256,1024]{1,0:T(8,128)(2,1)S(1)} %broadcast_multiply_fusion.x0, bf16[256,1024]{1,0:T(8,128)(2,1)} %collective-permute-done.2.x1, ...), custom_call_target="tpu_custom_call" | custom-call | flops 8589934592 | bytes 29360128 | tf_op jit(solution)/shard_map/update/pallas_call | solution.py:135
  (2 shorter events, 0.1 us)
Async XLA Ops:
  6.5 2.2 %copy-start = (bf16[1024,2048]{1,0:T(8,128)(2,1)S(1)}, bf16[1024,2048]{1,0:T(8,128)(2,1)}, u32[]{:S(2)}) copy-start(bf16[1024,2048]{1,0:T(8,128)(2,1)} %xc.1) | copy-start | bytes 12582916
  50.0 12.8 %collective-permute-start.1 = (bf16[128,1024]{1,0:T(8,128)(2,1)S(1)}, bf16[128,1024]{1,0:T(8,128)(2,1)S(1)}, u32[]{:S(2)}, u32[]{:S(2)}) collective-permute-start(bf16[128,1024]{1,0:T(8,128)(2,1)S(1)} %reduce_sum.12), channel_id=1, source_target_pairs={{0,0},{1,32},{2,64},{3,96},{4,16},{5,48},{6,80},{7,112},{8,8},{9,4... | collective-permute-start | bytes 786440 | tf_op jit(solution)/shard_map/ppermute | solution.py:182
  64.4 69.2 %all-to-all-start.1 = ((bf16[8,128,1024]{2,1,0:T(8,128)(2,1)}), bf16[8,128,1024]{2,1,0:T(8,128)(2,1)S(1)}, u32[]{:S(2)}, u32[]{:S(2)}) async-start(bf16[8,128,1024]{2,1,0:T(8,128)(2,1)} %broadcast_in_dim.2), calls=%async_computation.1 | async-start | bytes 4194304 | tf_op jit(solution)/shard_map/all_to_all | solution.py:43
  75.3 103.0 %all-gather.2.cloned.1.call-start = ((), (), s32[]{:S(2)}) async-start(), calls=%async_computation.2 | async-start | bytes 2621440 | tf_op jit(solution)/shard_map/all_gather | solution.py:186
  76.4 57.1 %collective-permute-start = (bf16[256,1024]{1,0:T(8,128)(2,1)S(1)}, bf16[256,1024]{1,0:T(8,128)(2,1)S(1)}, u32[]{:S(2)}, u32[]{:S(2)}) collective-permute-start(bf16[256,1024]{1,0:T(8,128)(2,1)S(1)} %dynamic_slice.3), channel_id=1, source_target_pairs={{0,0},{1,17},{2,34},{3,51},{4,68},{5,85},{6,102},{7,119},{8,8},{9,... | collective-permute-start | bytes 1572872 | tf_op jit(solution)/shard_map/ppermute | solution.py:174
  133.6 44.8 %collective-permute-start.5 = (bf16[1024,1024]{1,0:T(8,128)(2,1)S(1)}, bf16[1024,1024]{1,0:T(8,128)(2,1)}, u32[]{:S(2)}, u32[]{:S(2)}) collective-permute-start(bf16[1024,1024]{1,0:T(8,128)(2,1)S(1)} %bitcast.9), channel_id=1, source_target_pairs={{0,8},{8,0},{1,9},{9,1},{2,10},{10,2},{3,11},{11,3},{4,12},{12,4},... | collective-permute-start | bytes 6291464 | tf_op jit(solution)/shard_map/ppermute | solution.py:192
  134.5 20.1 %collective-permute-start.4 = (bf16[256,1024]{1,0:T(8,128)(2,1)S(1)}, bf16[256,1024]{1,0:T(8,128)(2,1)S(1)}, u32[]{:S(2)}, u32[]{:S(2)}) collective-permute-start(bf16[256,1024]{1,0:T(8,128)(2,1)S(1)} %broadcast_multiply_fusion.x0), channel_id=1, source_target_pairs={{0,2},{1,3},{2,0},{3,1},{4,6},{5,7},{6,4},{7,5},{8,10},{9,11},{10,... | collective-permute-start | bytes 1572872 | tf_op jit(solution)/shard_map/ppermute | solution.py:190
  134.5 26.4 %collective-permute-start.3 = (bf16[256,1024]{1,0:T(8,128)(2,1)S(1)}, bf16[256,1024]{1,0:T(8,128)(2,1)}, u32[]{:S(2)}, u32[]{:S(2)}) collective-permute-start(bf16[256,1024]{1,0:T(8,128)(2,1)S(1)} %broadcast_multiply_fusion.x0), channel_id=1, source_target_pairs={{0,3},{1,0},{2,1},{3,2},{4,7},{5,4},{6,5},{7,6},{8,11},{9,8},{10,9... | collective-permute-start | bytes 1572872 | tf_op jit(solution)/shard_map/ppermute | solution.py:190
  134.5 37.8 %collective-permute-start.2 = (bf16[256,1024]{1,0:T(8,128)(2,1)S(1)}, bf16[256,1024]{1,0:T(8,128)(2,1)}, u32[]{:S(2)}, u32[]{:S(2)}) collective-permute-start(bf16[256,1024]{1,0:T(8,128)(2,1)S(1)} %broadcast_multiply_fusion.x0), channel_id=1, source_target_pairs={{0,1},{1,2},{2,3},{3,0},{4,5},{5,6},{6,7},{7,4},{8,9},{9,10},{10,1... | collective-permute-start | bytes 1572872 | tf_op jit(solution)/shard_map/ppermute | solution.py:190
Sparse Core Ops, SparseCore 0:
  133.7 44.5 all-gather.1

commit v3 on v2

--- a/solution.py
+++ b/solution.py
@@ -1,4 +1,3 @@
-import functools
 import itertools
 
 import jax
@@ -26,7 +25,7 @@
 
 def crossing_of_sums():
     return [
-        (number(x, zl, h, zh, y), number(y, zh, h, x // 2, x % 2 * 2 + zl))
+        (number(x, zl, h, zh, y), number((x + y) % 4, zh, h, x // 2, x % 2 * 2 + zl))
         for x, zl, h, zh, y in places()
     ]
 
@@ -44,7 +43,7 @@
 
 
 TILE = 256
-STRIP = 512
+STRIP = 256
 
 
 def partial_kernel(samples, precision, out):
@@ -59,6 +58,8 @@
 def partial_sums(samples, precision):
     count, width = samples.shape
     rows = precision.shape[0]
+    samples = pltpu.with_memory_space_constraint(samples, pltpu.HBM)
+    precision = pltpu.with_memory_space_constraint(precision, pltpu.HBM)
     return pl.pallas_call(
         partial_kernel,
         out_shape=jax.ShapeDtypeStruct((count, rows), jnp.bfloat16),
@@ -77,13 +78,13 @@
 
 
 def update_kernel(
-    samples_count, whole, scalars, yr, x0, x1, x2, x3, xc, mine, other, precision, out, kept
+    whole, scales, steps, yr, x0, x1, x2, x3, xc, mine, other, precision, out, kept
 ):
     deep = x0.shape[0]
     t = pl.program_id(0)
     per_side = pl.num_programs(0) // 2
     contract = (((0,), (0,)), ((), ()))
-    step, level = scalars[0], scalars[1]
+    scale, step, level = scales[0], scales[1], steps[1]
 
     def finish(panel):
         total = lax.dot_general(yr[...], xc[...], contract, preferred_element_type=jnp.float32)
@@ -95,8 +96,7 @@
                 contract,
                 preferred_element_type=jnp.float32,
             )
-        gradient = total * (1.0 / samples_count)
-        stepped = precision[...] - step * gradient
+        stepped = precision[...] - scale * total
         out[...] = stepped - jnp.clip(stepped, -level, level)
         side = (whole[0] + t // per_side) % 2
         offset = whole[2] + (side * per_side + t % per_side) * TILE - whole[1]
@@ -121,7 +121,7 @@
         finish(other)
 
 
-def updated_tile(whole, scalars, yr, quarters, xc, mine, other, precision):
+def updated_tile(whole, scales, steps, yr, quarters, xc, mine, other, precision):
     rows, cols = precision.shape
     count = xc.shape[0]
     per_side = cols // TILE // 2
@@ -133,12 +133,13 @@
     tile = pl.BlockSpec((rows, TILE), column)
     yr = pltpu.with_memory_space_constraint(yr, pltpu.HBM)
     return pl.pallas_call(
-        functools.partial(update_kernel, count),
+        update_kernel,
         out_shape=jax.ShapeDtypeStruct(precision.shape, precision.dtype),
         grid_spec=pltpu.PrefetchScalarGridSpec(
             num_scalar_prefetch=1,
             grid=(2 * per_side,),
             in_specs=[
+                pl.BlockSpec(memory_space=pltpu.SMEM),
                 pl.BlockSpec(memory_space=pltpu.SMEM),
                 pl.BlockSpec(yr.shape, lambda t, whole: (0, 0)),
                 inside,
@@ -158,7 +159,13 @@
             flops=4 * rows * cols * count, bytes_accessed=28 << 20, transcendentals=0
         ),
         name="update",
-    )(whole, scalars, yr, *quarters, xc, mine, other, precision)
+    )(whole, scales, steps, yr, *quarters, xc, mine, other, precision)
+
+
+def joined(own, other, place):
+    upper = jnp.where(place == 0, own, other)
+    lower = jnp.where(place == 0, other, own)
+    return jnp.concatenate([upper, lower], axis=0)
 
 
 def per_device(precision, samples, step_size, threshold):
@@ -168,23 +175,26 @@
     parts = 8
     piece = sample_count // parts
 
-    mine = lax.dynamic_slice(
-        samples, ((x + y) % 4 * 2 * piece, h * rows_tile), (2 * piece, rows_tile)
-    )
-    own_quarter = lax.ppermute(mine, NAMES, crossing_of_samples())
+    block = (x + y) % 4 * 2 + (zl ^ zh)
+    mine = lax.dynamic_slice(samples, (block * piece, h * rows_tile), (piece, rows_tile))
+    own_eighth = lax.ppermute(mine, NAMES, crossing_of_samples())
     partial = partial_sums(samples, precision)
     shares = lax.all_to_all(partial.reshape(parts, piece, rows_tile), ("y", "zh"), 0, 0, tiled=True)
-    own_quarter = own_quarter * jnp.bfloat16(0.5)
+    own_eighth = own_eighth * jnp.bfloat16(0.5)
+    other_eighth = lax.ppermute(own_eighth, "zh", [(0, 1), (1, 0)])
+    steps = jnp.stack([step_size[0], step_size[0] * threshold[0]])
     total = jnp.sum(shares.astype(jnp.float32), axis=0)
     projected = total.astype(jnp.bfloat16)
     halved = projected * jnp.bfloat16(0.5)
 
     crossed = lax.ppermute(projected, NAMES, crossing_of_sums())
-    pair = lax.all_gather(halved, "zh", axis=0, tiled=True)
-    crossed, pair = lax.optimization_barrier((crossed, pair))
-    own_quarter, pair = lax.optimization_barrier((own_quarter, pair))
+    other = lax.ppermute(halved, "zh", [(0, 1), (1, 0)])
+    pair = joined(halved, other, zh)
+    later, _, pair = lax.optimization_barrier((step_size, threshold, pair))
     row_panel = lax.all_gather(pair, "y", axis=0, tiled=True)
+    own_quarter = joined(own_eighth, other_eighth, zh)
     quarters = [own_quarter]
+    scales = jnp.stack([later[0] * (1.0 / sample_count), later[0]])
     for turn in (1, 3, 2):
         moves = [(i, (i + turn) % 4) for i in range(4)]
         quarters.append(lax.ppermute(own_quarter, "y", moves))
@@ -193,11 +203,10 @@
 
     row_start = ((x * 2 + zl) * 2 + h) * rows_tile
     col_start = (zh * 4 + y) * cols_tile
-    places_of = [(y - turn) % 4 for turn in (0, 1, 3, 2)]
+    places_of = [(y - turn + zh * 2 + y // 2) % 4 for turn in (0, 1, 3, 2)]
     whole = jnp.stack([h, row_start, col_start, *places_of]).astype(jnp.int32)
-    scalars = jnp.stack([step_size[0], step_size[0] * threshold[0]])
     return updated_tile(
-        whole, scalars, row_panel, quarters, samples, panel, other_panel, precision
+        whole, scales, steps, row_panel, quarters, samples, panel, other_panel, precision
     )
 
 

time: 203 us -> 184 us (0.906)
  the two profiles are of different devices: /device:TPU:97 before, /device:TPU:0 now
where the time goes in v3:
time: 184 us; the launch traced here: 183 us
  waiting for transfers between devices  61.9 us (34%)
  starting transfers between devices  40.7 us (22%)
  blocking collectives  35.8 us (19%)
  Pallas kernels  25.8 us (14%)
  between operations  14.9 us (8%)
  local copies, waits for them, and re-layouts  2.64 us (1%)
    all_to_all x1, blocking collectives, per_device(): lax.all_to_all(partial.reshape(parts, piece, rows_tile), ('y', 'zh'), 0,...  35.8 us
    ppermute x1, waiting for transfers between devices, per_device(): other = lax.ppermute(halved, 'zh', [(0, 1), (1, 0)])  26.8 us
    ppermute x3, waiting for transfers between devices, per_device(): quarters.append(lax.ppermute(own_quarter, 'y', moves))  24 us
    pallas_call x1, Pallas kernels, updated_tile(): pl.pallas_call(update_kernel, out_shape=jax.ShapeDtypeStruct(precision.sh...  17.3 us
    all_to_all x1, starting transfers between devices, sent_to_all(): return lax.all_to_all(copies, axes, 0, 0, tiled=True)  17.1 us
    ppermute x1, starting transfers between devices, per_device(): other_eighth = lax.ppermute(own_eighth, 'zh', [(0, 1), (1, 0)])  11.3 us
    ppermute x1, waiting for transfers between devices, per_device(): other_eighth = lax.ppermute(own_eighth, 'zh', [(0, 1), (1, 0)])  11.1 us
    pallas_call x1, Pallas kernels, partial_sums(): pl.pallas_call(partial_kernel, out_shape=jax.ShapeDtypeStruct((count, row...  8.51 us
  transfers between devices with their start and end apart: 10, of which 4 were waited for; matrix products, arithmetic and copies ran while one was open for 1% of the time, Pallas kernels for 0%

profile of v3, /device:TPU:0, one launch (start us, length us, event | category | flops | bytes accessed | tf_op | source)
XLA Modules:
  0.0 183.2 jit_solution(12125024419146660794)
XLA Ops:
  6.5 8.5 %partial.1 = bf16[1024,1024]{1,0:T(8,128)(2,1)S(1)} custom-call(bf16[1024,2048]{1,0:T(8,128)(2,1)} %xc.1, f32[1024,2048]{1,0:T(8,128)} %precision.3), custom_call_target="tpu_custom_call" | custom-call | flops 4294967296 | bytes 14680064 | tf_op jit(solution)/shard_map/partial/pallas_call | solution.py:63
  15.0 35.8 %all_to_all.10 = bf16[8,128,1024]{2,1,0:T(8,128)(2,1)S(1)} all-to-all(bf16[8,128,1024]{2,1,0:T(8,128)(2,1)S(1)} %bitcast.11), channel_id=1, replica_groups=mesh['x'=4,'zl'=2,'core'=2,'zh'=2,'y'=4] {'y','zh'}, dimensions={0} | all-to-all | bytes 4194304 | tf_op jit(solution)/shard_map/all_to_all | solution.py:182
  50.8 0.4 reduce_sum.12
  51.2 0.7 collective-permute-start.6
  51.9 0.0 collective-permute-done.6
  51.9 1.6 broadcast_in_dim.2
  53.5 17.1 %all-to-all-start.1 = ((bf16[8,128,1024]{2,1,0:T(8,128)(2,1)}), bf16[8,128,1024]{2,1,0:T(8,128)(2,1)S(1)}, u32[]{:S(2)}, u32[]{:S(2)}) async-start(bf16[8,128,1024]{2,1,0:T(8,128)(2,1)} %broadcast_in_dim.2), calls=%async_computation.1 | async-start | bytes 4194304 | tf_op jit(solution)/shard_map/all_to_all | solution.py:42
  70.6 0.0 all-gather.2.cloned.1.call-start
  70.7 2.5 %collective-permute-start = (bf16[128,1024]{1,0:T(8,128)(2,1)S(1)}, bf16[128,1024]{1,0:T(8,128)(2,1)S(1)}, u32[]{:S(2)}, u32[]{:S(2)}) collective-permute-start(bf16[128,1024]{1,0:T(8,128)(2,1)S(1)} %broadcast_multiply_fusion.1), channel_id=1, source_target_pairs={{0,4},{4,0},{1,5},{5,1},{2,6},{6,2},{3,7},{7,3},{8,12},{12,8},{9,1... | collective-permute-start | bytes 786440 | tf_op jit(solution)/shard_map/ppermute | solution.py:191
  73.1 26.8 %collective-permute-done = bf16[128,1024]{1,0:T(8,128)(2,1)S(1)} collective-permute-done((bf16[128,1024]{1,0:T(8,128)(2,1)S(1)}, bf16[128,1024]{1,0:T(8,128)(2,1)S(1)}, u32[]{:S(2)}, u32[]{:S(2)}) %collective-permute-start) | collective-permute-done | bytes 262176 | tf_op jit(solution)/shard_map/ppermute | solution.py:191
  100.0 0.8 pad_maximum_fusion
  100.8 0.0 all-gather.2.cloned.1.call-update
  100.8 0.0 all-to-all-done.1
  100.8 0.1 collective-permute-start.7
  100.9 1.0 dynamic_slice.3
  101.9 0.7 collective-permute-start.1
  102.6 0.0 collective-permute-done.1
  102.6 11.3 %collective-permute-start.2 = (bf16[128,1024]{1,0:T(8,128)(2,1)S(1)}, bf16[128,1024]{1,0:T(8,128)(2,1)S(1)}, u32[]{:S(2)}, u32[]{:S(2)}) collective-permute-start(bf16[128,1024]{1,0:T(8,128)(2,1)S(1)} %broadcast_multiply_fusion), channel_id=1, source_target_pairs={{0,4},{4,0},{1,5},{5,1},{2,6},{6,2},{3,7},{7,3},{8,12},{12,8},{9,1... | collective-permute-start | bytes 786440 | tf_op jit(solution)/shard_map/ppermute | solution.py:184
  114.0 11.1 %collective-permute-done.2 = bf16[128,1024]{1,0:T(8,128)(2,1)S(1)} collective-permute-done((bf16[128,1024]{1,0:T(8,128)(2,1)S(1)}, bf16[128,1024]{1,0:T(8,128)(2,1)S(1)}, u32[]{:S(2)}, u32[]{:S(2)}) %collective-permute-start.2) | collective-permute-done | bytes 262176 | tf_op jit(solution)/shard_map/ppermute | solution.py:184
  125.2 4.9 %collective-permute-start.5 = (bf16[256,1024]{1,0:T(8,128)(2,1)S(1)}, bf16[256,1024]{1,0:T(8,128)(2,1)S(1)}, u32[]{:S(2)}, u32[]{:S(2)}) collective-permute-start(bf16[256,1024]{1,0:T(8,128)(2,1)S(1)} %pad_maximum_fusion.1.x0), channel_id=1, source_target_pairs={{0,2},{1,3},{2,0},{3,1},{4,6},{5,7},{6,4},{7,5},{8,10},{9,11},{10,... | collective-permute-start | bytes 1572872 | tf_op jit(solution)/shard_map/ppermute | solution.py:200
  130.1 2.6 %collective-permute-start.4 = (bf16[256,1024]{1,0:T(8,128)(2,1)S(1)}, bf16[256,1024]{1,0:T(8,128)(2,1)}, u32[]{:S(2)}, u32[]{:S(2)}) collective-permute-start(bf16[256,1024]{1,0:T(8,128)(2,1)S(1)} %pad_maximum_fusion.1.x0), channel_id=1, source_target_pairs={{0,3},{1,0},{2,1},{3,2},{4,7},{5,4},{6,5},{7,6},{8,11},{9,8},{10,9... | collective-permute-start | bytes 1572872 | tf_op jit(solution)/shard_map/ppermute | solution.py:200
  132.8 0.8 collective-permute-start.3
  134.9 0.1 stack.39.whole
  134.9 0.1 pad_maximum_fusion.2
  135.0 10.6 %collective-permute-done.5.x3 = bf16[256,1024]{1,0:T(8,128)(2,1)S(1)} collective-permute-done((bf16[256,1024]{1,0:T(8,128)(2,1)S(1)}, bf16[256,1024]{1,0:T(8,128)(2,1)S(1)}, u32[]{:S(2)}, u32[]{:S(2)}) %collective-permute-start.5) | collective-permute-done | bytes 524320 | tf_op jit(solution)/shard_map/ppermute | solution.py:200
  145.6 13.4 %collective-permute-done.4.x2 = bf16[256,1024]{1,0:T(8,128)(2,1)} collective-permute-done((bf16[256,1024]{1,0:T(8,128)(2,1)S(1)}, bf16[256,1024]{1,0:T(8,128)(2,1)}, u32[]{:S(2)}, u32[]{:S(2)}) %collective-permute-start.4) | collective-permute-done | bytes 524320 | tf_op jit(solution)/shard_map/ppermute | solution.py:200
  159.0 0.0 collective-permute-done.3.x1
  159.0 0.0 all-gather.2.cloned.1.call-done.yr
  159.0 0.0 collective-permute-done.7.other
  159.0 17.3 %update.1 = f32[1024,2048]{1,0:T(8,128)} custom-call(s32[7]{0:T(128)S(1)} %stack.39.whole, f32[2]{0:T(128)S(1)} %get-tuple-element.13.scales, f32[2]{0:T(128)S(1)} %get-tuple-element.14.steps, bf16[1024,1024]{1,0:T(8,128)(2,1)} %all-gather.2.cloned.1.call-done.yr, bf16[256,1024]{1,0:T(8,128)(2,1)S(1)} %pad_maximum_fusion.1.x0, ...), custom_call_target="tpu_custom_call" | custom-call | flops 8589934592 | bytes 29360128 | tf_op jit(solution)/shard_map/update/pallas_call | solution.py:135
  (5 shorter events, 0.2 us)
Async XLA Ops:
  51.2 0.7 collective-permute-start.6
  53.5 47.3 %all-to-all-start.1 = ((bf16[8,128,1024]{2,1,0:T(8,128)(2,1)}), bf16[8,128,1024]{2,1,0:T(8,128)(2,1)S(1)}, u32[]{:S(2)}, u32[]{:S(2)}) async-start(bf16[8,128,1024]{2,1,0:T(8,128)(2,1)} %broadcast_in_dim.2), calls=%async_computation.1 | async-start | bytes 4194304 | tf_op jit(solution)/shard_map/all_to_all | solution.py:42
  70.6 88.4 %all-gather.2.cloned.1.call-start = ((), (), s32[]{:S(2)}) async-start(), calls=%async_computation.2 | async-start | bytes 2621440 | tf_op jit(solution)/shard_map/all_gather | solution.py:194
  70.7 29.2 %collective-permute-start = (bf16[128,1024]{1,0:T(8,128)(2,1)S(1)}, bf16[128,1024]{1,0:T(8,128)(2,1)S(1)}, u32[]{:S(2)}, u32[]{:S(2)}) collective-permute-start(bf16[128,1024]{1,0:T(8,128)(2,1)S(1)} %broadcast_multiply_fusion.1), channel_id=1, source_target_pairs={{0,4},{4,0},{1,5},{5,1},{2,6},{6,2},{3,7},{7,3},{8,12},{12,8},{9,1... | collective-permute-start | bytes 786440 | tf_op jit(solution)/shard_map/ppermute | solution.py:191
  100.8 58.2 %collective-permute-start.7 = (bf16[1024,1024]{1,0:T(8,128)(2,1)S(1)}, bf16[1024,1024]{1,0:T(8,128)(2,1)}, u32[]{:S(2)}, u32[]{:S(2)}) collective-permute-start(bf16[1024,1024]{1,0:T(8,128)(2,1)S(1)} %bitcast.9), channel_id=1, source_target_pairs={{0,8},{8,0},{1,9},{9,1},{2,10},{10,2},{3,11},{11,3},{4,12},{12,4},... | collective-permute-start | bytes 6291464 | tf_op jit(solution)/shard_map/ppermute | solution.py:202
  101.9 0.7 collective-permute-start.1
  102.6 22.5 %collective-permute-start.2 = (bf16[128,1024]{1,0:T(8,128)(2,1)S(1)}, bf16[128,1024]{1,0:T(8,128)(2,1)S(1)}, u32[]{:S(2)}, u32[]{:S(2)}) collective-permute-start(bf16[128,1024]{1,0:T(8,128)(2,1)S(1)} %broadcast_multiply_fusion), channel_id=1, source_target_pairs={{0,4},{4,0},{1,5},{5,1},{2,6},{6,2},{3,7},{7,3},{8,12},{12,8},{9,1... | collective-permute-start | bytes 786440 | tf_op jit(solution)/shard_map/ppermute | solution.py:184
  125.2 20.4 %collective-permute-start.5 = (bf16[256,1024]{1,0:T(8,128)(2,1)S(1)}, bf16[256,1024]{1,0:T(8,128)(2,1)S(1)}, u32[]{:S(2)}, u32[]{:S(2)}) collective-permute-start(bf16[256,1024]{1,0:T(8,128)(2,1)S(1)} %pad_maximum_fusion.1.x0), channel_id=1, source_target_pairs={{0,2},{1,3},{2,0},{3,1},{4,6},{5,7},{6,4},{7,5},{8,10},{9,11},{10,... | collective-permute-start | bytes 1572872 | tf_op jit(solution)/shard_map/ppermute | solution.py:200
  130.1 28.9 %collective-permute-start.4 = (bf16[256,1024]{1,0:T(8,128)(2,1)S(1)}, bf16[256,1024]{1,0:T(8,128)(2,1)}, u32[]{:S(2)}, u32[]{:S(2)}) collective-permute-start(bf16[256,1024]{1,0:T(8,128)(2,1)S(1)} %pad_maximum_fusion.1.x0), channel_id=1, source_target_pairs={{0,3},{1,0},{2,1},{3,2},{4,7},{5,4},{6,5},{7,6},{8,11},{9,8},{10,9... | collective-permute-start | bytes 1572872 | tf_op jit(solution)/shard_map/ppermute | solution.py:200
  132.8 26.2 %collective-permute-start.3 = (bf16[256,1024]{1,0:T(8,128)(2,1)S(1)}, bf16[256,1024]{1,0:T(8,128)(2,1)}, u32[]{:S(2)}, u32[]{:S(2)}) collective-permute-start(bf16[256,1024]{1,0:T(8,128)(2,1)S(1)} %pad_maximum_fusion.1.x0), channel_id=1, source_target_pairs={{0,1},{1,2},{2,3},{3,0},{4,5},{5,6},{6,7},{7,4},{8,9},{9,10},{10,1... | collective-permute-start | bytes 1572872 | tf_op jit(solution)/shard_map/ppermute | solution.py:200
Sparse Core Ops, SparseCore 0:
  100.9 47.5 all-gather.1

commit v4 on v3

--- a/solution.py
+++ b/solution.py
@@ -78,24 +78,28 @@
 
 
 def update_kernel(
-    whole, scales, steps, yr, x0, x1, x2, x3, xc, mine, other, precision, out, kept
+    whole, scales, steps, y0, y1, y2, y3, x0, x1, x2, x3, xc, mine, other, precision, out, kept
 ):
     deep = x0.shape[0]
     t = pl.program_id(0)
     per_side = pl.num_programs(0) // 2
-    contract = (((0,), (0,)), ((), ()))
     scale, step, level = scales[0], scales[1], steps[1]
 
-    def finish(panel):
-        total = lax.dot_general(yr[...], xc[...], contract, preferred_element_type=jnp.float32)
-        for d, quarter in enumerate((x0, x1, x2, x3)):
-            start = pl.multiple_of(whole[3 + d] * deep, deep)
-            total = total + lax.dot_general(
+    def product(quarters, panel, first_place):
+        total = None
+        for d, quarter in enumerate(quarters):
+            start = pl.multiple_of(whole[first_place + d] * deep, deep)
+            term = lax.dot_general(
                 quarter[...],
                 panel[pl.ds(start, deep), :],
-                contract,
+                (((0,), (0,)), ((), ())),
                 preferred_element_type=jnp.float32,
             )
+            total = term if total is None else total + term
+        return total
+
+    def finish(panel):
+        total = product((x0, x1, x2, x3), panel, 7) + product((y0, y1, y2, y3), xc, 3)
         stepped = precision[...] - scale * total
         out[...] = stepped - jnp.clip(stepped, -level, level)
         side = (whole[0] + t // per_side) % 2
@@ -121,7 +125,7 @@
         finish(other)
 
 
-def updated_tile(whole, scales, steps, yr, quarters, xc, mine, other, precision):
+def updated_tile(whole, scales, steps, row_quarters, quarters, xc, mine, other, precision):
     rows, cols = precision.shape
     count = xc.shape[0]
     per_side = cols // TILE // 2
@@ -131,7 +135,6 @@
         return 0, (whole[0] + t // per_side) % 2 * per_side + t % per_side
 
     tile = pl.BlockSpec((rows, TILE), column)
-    yr = pltpu.with_memory_space_constraint(yr, pltpu.HBM)
     return pl.pallas_call(
         update_kernel,
         out_shape=jax.ShapeDtypeStruct(precision.shape, precision.dtype),
@@ -141,11 +144,7 @@
             in_specs=[
                 pl.BlockSpec(memory_space=pltpu.SMEM),
                 pl.BlockSpec(memory_space=pltpu.SMEM),
-                pl.BlockSpec(yr.shape, lambda t, whole: (0, 0)),
-                inside,
-                inside,
-                inside,
-                inside,
+                *[inside] * 8,
                 pl.BlockSpec((count, TILE), column),
                 pl.BlockSpec((count, TILE), lambda t, whole: (0, jnp.minimum(t, per_side - 1))),
                 pl.BlockSpec((count, TILE), lambda t, whole: (0, jnp.maximum(t - per_side, 0))),
@@ -159,7 +158,16 @@
             flops=4 * rows * cols * count, bytes_accessed=28 << 20, transcendentals=0
         ),
         name="update",
-    )(whole, scales, steps, yr, *quarters, xc, mine, other, precision)
+    )(whole, scales, steps, *row_quarters, *quarters, xc, mine, other, precision)
+
+
+TURNS = (0, 1, 3, 2)
+
+
+def spread_along_y(quarter):
+    return [quarter] + [
+        lax.ppermute(quarter, "y", [(i, (i + turn) % 4) for i in range(4)]) for turn in TURNS[1:]
+    ]
 
 
 def joined(own, other, place):
@@ -191,22 +199,20 @@
     other = lax.ppermute(halved, "zh", [(0, 1), (1, 0)])
     pair = joined(halved, other, zh)
     later, _, pair = lax.optimization_barrier((step_size, threshold, pair))
-    row_panel = lax.all_gather(pair, "y", axis=0, tiled=True)
+    row_quarters = spread_along_y(pair)
     own_quarter = joined(own_eighth, other_eighth, zh)
-    quarters = [own_quarter]
+    quarters = spread_along_y(own_quarter)
     scales = jnp.stack([later[0] * (1.0 / sample_count), later[0]])
-    for turn in (1, 3, 2):
-        moves = [(i, (i + turn) % 4) for i in range(4)]
-        quarters.append(lax.ppermute(own_quarter, "y", moves))
     panel = sent_to_all(crossed, ("x", "zl"), parts).reshape(sample_count, rows_tile)
     other_panel = lax.ppermute(panel, "core", [(0, 1), (1, 0)])
 
     row_start = ((x * 2 + zl) * 2 + h) * rows_tile
     col_start = (zh * 4 + y) * cols_tile
-    places_of = [(y - turn + zh * 2 + y // 2) % 4 for turn in (0, 1, 3, 2)]
+    places_of = [(y - turn) % 4 for turn in TURNS]
+    places_of += [(place + zh * 2 + y // 2) % 4 for place in places_of]
     whole = jnp.stack([h, row_start, col_start, *places_of]).astype(jnp.int32)
     return updated_tile(
-        whole, scales, steps, row_panel, quarters, samples, panel, other_panel, precision
+        whole, scales, steps, row_quarters, quarters, samples, panel, other_panel, precision
     )
 
 

time: 184 us -> 176 us (0.957)
  waiting for transfers between devices: 61.9 us -> 76.4 us
  between operations: 14.9 us -> 1.41 us
  starting transfers between devices: 40.7 us -> 32.3 us
    all_to_all x1, waiting for transfers between devices: 0.01 us -> 29.6 us  [sent_to_all(): return lax.all_to_all(copies, axes, 0, 0, tiled=True)]
    ppermute x1, waiting for transfers between devices: 26.8 us -> 1.35 us  [per_device(): other = lax.ppermute(halved, 'zh', [(0, 1), (1, 0)])]
    ppermute x3 -> x6, waiting for transfers between devices: 24 us -> 35.4 us  [spread_along_y(): lax.ppermute(quarter, 'y', [(i, (i + turn) % 4) for i in range(4)])]
    ppermute x1, starting transfers between devices: 11.3 us -> 0.29 us  [per_device(): other_eighth = lax.ppermute(own_eighth, 'zh', [(0, 1), (1, 0)])]
    ppermute x3 -> x6, starting transfers between devices: 8.34 us -> 10.4 us  [spread_along_y(): lax.ppermute(quarter, 'y', [(i, (i + turn) % 4) for i in range(4)])]
  transfers between devices with their start and end apart: 10 -> 12, of which waited for: 4 -> 8; matrix products, arithmetic and copies ran while one was open for 1% -> 1% of each run, Pallas kernels for 0% -> 0%
where the time goes in v4:
time: 176 us; the launch traced here: 175 us
  waiting for transfers between devices  76.4 us (43%)
  blocking collectives  35.8 us (20%)
  starting transfers between devices  32.3 us (18%)
  Pallas kernels  25.7 us (15%)
  local copies, waits for them, and re-layouts  2.64 us (2%)
    all_to_all x1, blocking collectives, per_device(): lax.all_to_all(partial.reshape(parts, piece, rows_tile), ('y', 'zh'), 0,...  35.8 us
    ppermute x6, waiting for transfers between devices, spread_along_y(): lax.ppermute(quarter, 'y', [(i, (i + turn) % 4) for i in range(4)])  35.4 us
    all_to_all x1, waiting for transfers between devices, sent_to_all(): return lax.all_to_all(copies, axes, 0, 0, tiled=True)  29.6 us
    pallas_call x1, Pallas kernels, updated_tile(): pl.pallas_call(update_kernel, out_shape=jax.ShapeDtypeStruct(precision.sh...  17.2 us
    all_to_all x1, starting transfers between devices, sent_to_all(): return lax.all_to_all(copies, axes, 0, 0, tiled=True)  17.1 us
    ppermute x6, starting transfers between devices, spread_along_y(): lax.ppermute(quarter, 'y', [(i, (i + turn) % 4) for i in range(4)])  10.4 us
    ppermute x1, waiting for transfers between devices, per_device(): other_eighth = lax.ppermute(own_eighth, 'zh', [(0, 1), (1, 0)])  10 us
    pallas_call x1, Pallas kernels, partial_sums(): pl.pallas_call(partial_kernel, out_shape=jax.ShapeDtypeStruct((count, row...  8.51 us
  transfers between devices with their start and end apart: 12, of which 8 were waited for; matrix products, arithmetic and copies ran while one was open for 1% of the time, Pallas kernels for 0%

profile of v4, /device:TPU:0, one launch (start us, length us, event | category | flops | bytes accessed | tf_op | source)
XLA Modules:
  0.0 174.8 jit_solution(7154532929713227312)
XLA Ops:
  0.0 8.5 %partial.1 = bf16[1024,1024]{1,0:T(8,128)(2,1)S(1)} custom-call(bf16[1024,2048]{1,0:T(8,128)(2,1)} %xc.1, f32[1024,2048]{1,0:T(8,128)} %precision.3), custom_call_target="tpu_custom_call" | custom-call | flops 4294967296 | bytes 14680064 | tf_op jit(solution)/shard_map/partial/pallas_call | solution.py:63
  8.5 35.8 %all_to_all.10 = bf16[8,128,1024]{2,1,0:T(8,128)(2,1)S(1)} all-to-all(bf16[8,128,1024]{2,1,0:T(8,128)(2,1)S(1)} %bitcast.13), channel_id=1, replica_groups=mesh['x'=4,'zl'=2,'core'=2,'zh'=2,'y'=4] {'y','zh'}, dimensions={0} | all-to-all | bytes 4194304 | tf_op jit(solution)/shard_map/all_to_all | solution.py:190
  44.3 0.4 reduce_sum.12
  44.7 0.7 collective-permute-start.9
  45.4 0.0 collective-permute-done.9
  45.4 1.6 broadcast_in_dim.2
  46.9 17.1 %all-to-all-start.1 = ((bf16[8,128,1024]{2,1,0:T(8,128)(2,1)}), bf16[8,128,1024]{2,1,0:T(8,128)(2,1)}, u32[]{:S(2)}, u32[]{:S(2)}) async-start(bf16[8,128,1024]{2,1,0:T(8,128)(2,1)} %broadcast_in_dim.2), calls=%async_computation.1 | async-start | bytes 4194304 | tf_op jit(solution)/shard_map/all_to_all | solution.py:42
  64.1 1.0 dynamic_slice.3
  65.0 0.7 collective-permute-start.4
  65.7 29.6 %all-to-all-done.1 = bf16[8,128,1024]{2,1,0:T(8,128)(2,1)} async-done(((bf16[8,128,1024]{2,1,0:T(8,128)(2,1)}), bf16[8,128,1024]{2,1,0:T(8,128)(2,1)}, u32[]{:S(2)}, u32[]{:S(2)}) %all-to-all-start.1) | async-done | bytes 2097184 | tf_op jit(solution)/shard_map/all_to_all | solution.py:42
  95.4 0.0 collective-permute-start.10
  95.4 0.0 collective-permute-done.4
  95.4 0.3 collective-permute-start.5
  95.7 10.0 %collective-permute-done.5 = bf16[128,1024]{1,0:T(8,128)(2,1)S(1)} collective-permute-done((bf16[128,1024]{1,0:T(8,128)(2,1)S(1)}, bf16[128,1024]{1,0:T(8,128)(2,1)S(1)}, u32[]{:S(2)}, u32[]{:S(2)}) %collective-permute-start.5) | collective-permute-done | bytes 262176 | tf_op jit(solution)/shard_map/ppermute | solution.py:192
  105.8 3.1 %collective-permute-start = (bf16[128,1024]{1,0:T(8,128)(2,1)S(1)}, bf16[128,1024]{1,0:T(8,128)(2,1)S(1)}, u32[]{:S(2)}, u32[]{:S(2)}) collective-permute-start(bf16[128,1024]{1,0:T(8,128)(2,1)S(1)} %broadcast_multiply_fusion.1), channel_id=1, source_target_pairs={{0,4},{4,0},{1,5},{5,1},{2,6},{6,2},{3,7},{7,3},{8,12},{12,8},{9,1... | collective-permute-start | bytes 786440 | tf_op jit(solution)/shard_map/ppermute | solution.py:199
  108.9 0.2 collective-permute-start.8
  109.1 4.0 %collective-permute-start.7 = (bf16[256,1024]{1,0:T(8,128)(2,1)S(1)}, bf16[256,1024]{1,0:T(8,128)(2,1)S(1)}, u32[]{:S(2)}, u32[]{:S(2)}) collective-permute-start(bf16[256,1024]{1,0:T(8,128)(2,1)S(1)} %pad_maximum_fusion.1.x0), channel_id=1, source_target_pairs={{0,3},{1,0},{2,1},{3,2},{4,7},{5,4},{6,5},{7,6},{8,11},{9,8},{10,9... | collective-permute-start | bytes 1572872 | tf_op jit(solution)/shard_map/ppermute | solution.py:169
  113.1 0.8 collective-permute-start.6
  113.9 1.3 collective-permute-done
  115.3 1.4 collective-permute-start.3
  116.7 8.6 %collective-permute-done.8.x3 = bf16[256,1024]{1,0:T(8,128)(2,1)S(1)} collective-permute-done((bf16[256,1024]{1,0:T(8,128)(2,1)S(1)}, bf16[256,1024]{1,0:T(8,128)(2,1)S(1)}, u32[]{:S(2)}, u32[]{:S(2)}) %collective-permute-start.8) | collective-permute-done | bytes 524320 | tf_op jit(solution)/shard_map/ppermute | solution.py:169
  125.3 4.0 %collective-permute-start.2 = (bf16[256,1024]{1,0:T(8,128)(2,1)S(1)}, bf16[256,1024]{1,0:T(8,128)(2,1)}, u32[]{:S(2)}, u32[]{:S(2)}) collective-permute-start(bf16[256,1024]{1,0:T(8,128)(2,1)S(1)} %pad_maximum_fusion.y0), channel_id=1, source_target_pairs={{0,3},{1,0},{2,1},{3,2},{4,7},{5,4},{6,5},{7,6},{8,11},{9,8},{10,9... | collective-permute-start | bytes 1572872 | tf_op jit(solution)/shard_map/ppermute | solution.py:169
  129.3 8.6 %collective-permute-done.7.x2 = bf16[256,1024]{1,0:T(8,128)(2,1)S(1)} collective-permute-done((bf16[256,1024]{1,0:T(8,128)(2,1)S(1)}, bf16[256,1024]{1,0:T(8,128)(2,1)S(1)}, u32[]{:S(2)}, u32[]{:S(2)}) %collective-permute-start.7) | collective-permute-done | bytes 524320 | tf_op jit(solution)/shard_map/ppermute | solution.py:169
  137.9 0.1 collective-permute-start.1
  139.3 0.1 stack.55.whole
  139.4 0.1 pad_maximum_fusion.2
  139.4 0.0 collective-permute-done.6.x1
  139.4 8.4 %collective-permute-done.3.y3 = bf16[256,1024]{1,0:T(8,128)(2,1)S(1)} collective-permute-done((bf16[256,1024]{1,0:T(8,128)(2,1)S(1)}, bf16[256,1024]{1,0:T(8,128)(2,1)S(1)}, u32[]{:S(2)}, u32[]{:S(2)}) %collective-permute-start.3) | collective-permute-done | bytes 524320 | tf_op jit(solution)/shard_map/ppermute | solution.py:169
  147.9 9.2 %collective-permute-done.2.y2 = bf16[256,1024]{1,0:T(8,128)(2,1)} collective-permute-done((bf16[256,1024]{1,0:T(8,128)(2,1)S(1)}, bf16[256,1024]{1,0:T(8,128)(2,1)}, u32[]{:S(2)}, u32[]{:S(2)}) %collective-permute-start.2) | collective-permute-done | bytes 524320 | tf_op jit(solution)/shard_map/ppermute | solution.py:169
  157.0 0.6 collective-permute-done.1.y1
  157.6 0.0 collective-permute-done.10.other
  157.6 17.2 %update.1 = f32[1024,2048]{1,0:T(8,128)} custom-call(s32[11]{0:T(128)S(1)} %stack.55.whole, f32[2]{0:T(128)S(1)} %get-tuple-element.13.scales, f32[2]{0:T(128)S(1)} %get-tuple-element.14.steps, bf16[256,1024]{1,0:T(8,128)(2,1)S(1)} %pad_maximum_fusion.y0, bf16[256,1024]{1,0:T(8,128)(2,1)} %collective-permute-done.1.y1, ...), custom_call_target="tpu_custom_call" | custom-call | flops 8589934592 | bytes 29360128 | tf_op jit(solution)/shard_map/update/pallas_call | solution.py:138
  (6 shorter events, 0.2 us)
Async XLA Ops:
  44.7 0.7 collective-permute-start.9
  46.9 48.4 %all-to-all-start.1 = ((bf16[8,128,1024]{2,1,0:T(8,128)(2,1)}), bf16[8,128,1024]{2,1,0:T(8,128)(2,1)}, u32[]{:S(2)}, u32[]{:S(2)}) async-start(bf16[8,128,1024]{2,1,0:T(8,128)(2,1)} %broadcast_in_dim.2), calls=%async_computation.1 | async-start | bytes 4194304 | tf_op jit(solution)/shard_map/all_to_all | solution.py:42
  65.0 30.3 %collective-permute-start.4 = (bf16[128,1024]{1,0:T(8,128)(2,1)S(1)}, bf16[128,1024]{1,0:T(8,128)(2,1)S(1)}, u32[]{:S(2)}, u32[]{:S(2)}) collective-permute-start(bf16[128,1024]{1,0:T(8,128)(2,1)S(1)} %dynamic_slice.3), channel_id=1, source_target_pairs={{0,0},{1,17},{2,34},{3,51},{4,68},{5,85},{6,102},{7,119},{8,8},{9,... | collective-permute-start | bytes 786440 | tf_op jit(solution)/shard_map/ppermute | solution.py:188
  95.4 62.3 %collective-permute-start.10 = (bf16[1024,1024]{1,0:T(8,128)(2,1)}, bf16[1024,1024]{1,0:T(8,128)(2,1)}, u32[]{:S(2)}, u32[]{:S(2)}) collective-permute-start(bf16[1024,1024]{1,0:T(8,128)(2,1)} %bitcast.12.mine), channel_id=1, source_target_pairs={{0,8},{8,0},{1,9},{9,1},{2,10},{10,2},{3,11},{11,3},{4,12},{12,4},... | collective-permute-start | bytes 6291464 | tf_op jit(solution)/shard_map/ppermute | solution.py:207
  95.4 10.3 %collective-permute-start.5 = (bf16[128,1024]{1,0:T(8,128)(2,1)S(1)}, bf16[128,1024]{1,0:T(8,128)(2,1)S(1)}, u32[]{:S(2)}, u32[]{:S(2)}) collective-permute-start(bf16[128,1024]{1,0:T(8,128)(2,1)S(1)} %broadcast_multiply_fusion), channel_id=1, source_target_pairs={{0,4},{4,0},{1,5},{5,1},{2,6},{6,2},{3,7},{7,3},{8,12},{12,8},{9,1... | collective-permute-start | bytes 786440 | tf_op jit(solution)/shard_map/ppermute | solution.py:192
  105.8 9.4 %collective-permute-start = (bf16[128,1024]{1,0:T(8,128)(2,1)S(1)}, bf16[128,1024]{1,0:T(8,128)(2,1)S(1)}, u32[]{:S(2)}, u32[]{:S(2)}) collective-permute-start(bf16[128,1024]{1,0:T(8,128)(2,1)S(1)} %broadcast_multiply_fusion.1), channel_id=1, source_target_pairs={{0,4},{4,0},{1,5},{5,1},{2,6},{6,2},{3,7},{7,3},{8,12},{12,8},{9,1... | collective-permute-start | bytes 786440 | tf_op jit(solution)/shard_map/ppermute | solution.py:199
  108.9 16.4 %collective-permute-start.8 = (bf16[256,1024]{1,0:T(8,128)(2,1)S(1)}, bf16[256,1024]{1,0:T(8,128)(2,1)S(1)}, u32[]{:S(2)}, u32[]{:S(2)}) collective-permute-start(bf16[256,1024]{1,0:T(8,128)(2,1)S(1)} %pad_maximum_fusion.1.x0), channel_id=1, source_target_pairs={{0,2},{1,3},{2,0},{3,1},{4,6},{5,7},{6,4},{7,5},{8,10},{9,11},{10,... | collective-permute-start | bytes 1572872 | tf_op jit(solution)/shard_map/ppermute | solution.py:169
  109.1 28.8 %collective-permute-start.7 = (bf16[256,1024]{1,0:T(8,128)(2,1)S(1)}, bf16[256,1024]{1,0:T(8,128)(2,1)S(1)}, u32[]{:S(2)}, u32[]{:S(2)}) collective-permute-start(bf16[256,1024]{1,0:T(8,128)(2,1)S(1)} %pad_maximum_fusion.1.x0), channel_id=1, source_target_pairs={{0,3},{1,0},{2,1},{3,2},{4,7},{5,4},{6,5},{7,6},{8,11},{9,8},{10,9... | collective-permute-start | bytes 1572872 | tf_op jit(solution)/shard_map/ppermute | solution.py:169
  113.1 26.3 %collective-permute-start.6 = (bf16[256,1024]{1,0:T(8,128)(2,1)S(1)}, bf16[256,1024]{1,0:T(8,128)(2,1)S(1)}, u32[]{:S(2)}, u32[]{:S(2)}) collective-permute-start(bf16[256,1024]{1,0:T(8,128)(2,1)S(1)} %pad_maximum_fusion.1.x0), channel_id=1, source_target_pairs={{0,1},{1,2},{2,3},{3,0},{4,5},{5,6},{6,7},{7,4},{8,9},{9,10},{10,1... | collective-permute-start | bytes 1572872 | tf_op jit(solution)/shard_map/ppermute | solution.py:169
  115.3 32.6 %collective-permute-start.3 = (bf16[256,1024]{1,0:T(8,128)(2,1)S(1)}, bf16[256,1024]{1,0:T(8,128)(2,1)S(1)}, u32[]{:S(2)}, u32[]{:S(2)}) collective-permute-start(bf16[256,1024]{1,0:T(8,128)(2,1)S(1)} %pad_maximum_fusion.y0), channel_id=1, source_target_pairs={{0,2},{1,3},{2,0},{3,1},{4,6},{5,7},{6,4},{7,5},{8,10},{9,11},{10,... | collective-permute-start | bytes 1572872 | tf_op jit(solution)/shard_map/ppermute | solution.py:169
  125.3 31.7 %collective-permute-start.2 = (bf16[256,1024]{1,0:T(8,128)(2,1)S(1)}, bf16[256,1024]{1,0:T(8,128)(2,1)}, u32[]{:S(2)}, u32[]{:S(2)}) collective-permute-start(bf16[256,1024]{1,0:T(8,128)(2,1)S(1)} %pad_maximum_fusion.y0), channel_id=1, source_target_pairs={{0,3},{1,0},{2,1},{3,2},{4,7},{5,4},{6,5},{7,6},{8,11},{9,8},{10,9... | collective-permute-start | bytes 1572872 | tf_op jit(solution)/shard_map/ppermute | solution.py:169
  137.9 19.8 %collective-permute-start.1 = (bf16[256,1024]{1,0:T(8,128)(2,1)S(1)}, bf16[256,1024]{1,0:T(8,128)(2,1)}, u32[]{:S(2)}, u32[]{:S(2)}) collective-permute-start(bf16[256,1024]{1,0:T(8,128)(2,1)S(1)} %pad_maximum_fusion.y0), channel_id=1, source_target_pairs={{0,1},{1,2},{2,3},{3,0},{4,5},{5,6},{6,7},{7,4},{8,9},{9,10},{10,1... | collective-permute-start | bytes 1572872 | tf_op jit(solution)/shard_map/ppermute | solution.py:169

commit v5 on v4

v5 whole, which is shorter than its diff:
```python
import itertools

import jax
import jax.numpy as jnp
from jax import lax
from jax.experimental import pallas as pl
from jax.experimental.pallas import tpu as pltpu
from jax.sharding import Mesh
from jax.sharding import PartitionSpec as P


SIZES = (4, 2, 2, 2, 4)
NAMES = ("x", "zl", "core", "zh", "y")
ROW = ("x", "zl", "core")
COL = ("zh", "y")


def number(x, zl, h, zh, y):
    return (((x * 2 + zl) * 2 + h) * 2 + zh) * 4 + y


def places():
    return itertools.product(*(range(n) for n in SIZES))


def crossing_of_sums():
    return [
        (number(x, zl, h, zh, y), number((x + y) % 4, zh, h, x // 2, x % 2 * 2 + zl))
        for x, zl, h, zh, y in places()
    ]


def crossing_of_samples():
    return [
        (number(x, zl, h, zh, y), number(zh * 2 + y // 2, y % 2, h, zl ^ zh, (x + y) % 4))
        for x, zl, h, zh, y in places()
    ]


def sent_to_all(array, axes, length):
    copies = jnp.broadcast_to(array[None], (length, *array.shape))
    return lax.all_to_all(copies, axes, 0, 0, tiled=True)


TILE = 256
STRIP = 256


def partial_kernel(samples, precision, out):
    out[...] = lax.dot_general(
        samples[...],
        precision[...].astype(jnp.bfloat16),
        (((1,), (1,)), ((), ())),
        preferred_element_type=jnp.float32,
    ).astype(jnp.bfloat16)


def partial_sums(samples, precision):
    count, width = samples.shape
    rows = precision.shape[0]
    samples = pltpu.with_memory_space_constraint(samples, pltpu.HBM)
    precision = pltpu.with_memory_space_constraint(precision, pltpu.HBM)
    return pl.pallas_call(
        partial_kernel,
        out_shape=jax.ShapeDtypeStruct((count, rows), jnp.bfloat16),
        grid=(rows // STRIP,),
        in_specs=[
            pl.BlockSpec((count, width), lambda r: (0, 0)),
            pl.BlockSpec((STRIP, width), lambda r: (r, 0)),
        ],
        out_specs=pl.BlockSpec((count, STRIP), lambda r: (0, r)),
        compiler_params=pltpu.CompilerParams(vmem_limit_bytes=40 << 20),
        cost_estimate=pl.CostEstimate(
            flops=2 * count * rows * width, bytes_accessed=14 << 20, transcendentals=0
        ),
        name="partial",
    )(samples, precision)


CONTRACT = (((0,), (0,)), ((), ()))


def in_hbm(*arrays):
    return [pltpu.with_memory_space_constraint(a, pltpu.HBM) for a in arrays]


def sum_of_products(whole, first_place, quarters, panel):
    total = None
    for d, quarter in enumerate(quarters):
        deep = quarter.shape[0]
        start = pl.multiple_of(whole[first_place + d] * deep, deep)
        term = lax.dot_general(
            quarter, panel[pl.ds(start, deep), :], CONTRACT, preferred_element_type=jnp.float32
        )
        total = term if total is None else total + term
    return total


def update_kernel(
    whole, scales, steps, y0, y1, y2, y3, y4, x0, x1, x2, x3, x4, xc, panel, precision, *rest
):
    out, kept = rest[-2:]
    t = pl.program_id(0)
    scale, step, level = scales[0], scales[1], steps[1]
    opposite = jnp.concatenate([y3[...], y4[...]], axis=0)
    total = sum_of_products(whole, 3, (y0[...], y1[...], y2[...], opposite), xc)
    turned = jnp.concatenate([x3[...], x4[...]], axis=0)
    total = total + sum_of_products(whole, 7, (x0[...], x1[...], x2[...], turned), panel)
    stepped = precision[...] - scale * total
    out[...] = stepped - jnp.clip(stepped, -level, level)
    offset = whole[2] + (whole[0] * pl.num_programs(0) + t) * TILE - whole[1]

    @pl.when((offset >= 0) & (offset < out.shape[0]))
    def _():
        kept[...] = stepped
        rows = pl.ds(pl.multiple_of(offset, TILE), TILE)
        own, shrunk = precision[rows, :], out[rows, :]
        on_diagonal = lax.broadcasted_iota(jnp.int32, own.shape, 0) == (
            lax.broadcasted_iota(jnp.int32, own.shape, 1)
        )
        raised = kept[rows, :] + step / jnp.where(on_diagonal, own, 1.0)
        out[rows, :] = jnp.where(on_diagonal, raised, shrunk)


def updated_half(whole, scales, steps, row_quarters, quarters, xc, panel, precision, into):
    rows, _ = precision.shape
    count, width = panel.shape
    per_side = width // TILE
    inside = pl.BlockSpec(memory_space=pltpu.VMEM)
    scalar = pl.BlockSpec(memory_space=pltpu.SMEM)
    tile = pl.BlockSpec((rows, TILE), lambda t, whole: (0, whole[0] * per_side + t))
    xc, precision = in_hbm(xc, precision)
    arrays = [whole, scales, steps, *row_quarters, *quarters, xc, panel, precision]
    specs = [scalar] * 2 + [inside] * 10
    specs += [
        pl.BlockSpec((count, TILE), lambda t, whole: (0, whole[0] * per_side + t)),
        pl.BlockSpec((count, TILE), lambda t, whole: (0, t)),
        tile,
    ]
    aliases = {}
    if into is not None:
        aliases = {len(arrays): 0}
        arrays.append(into)
        specs.append(pl.BlockSpec(memory_space=pl.ANY))
    return pl.pallas_call(
        update_kernel,
        out_shape=jax.ShapeDtypeStruct(precision.shape, precision.dtype),
        grid_spec=pltpu.PrefetchScalarGridSpec(
            num_scalar_prefetch=1,
            grid=(per_side,),
            in_specs=specs,
            out_specs=tile,
            scratch_shapes=[pltpu.VMEM((rows, TILE), jnp.float32)],
        ),
        input_output_aliases=aliases,
        compiler_params=pltpu.CompilerParams(vmem_limit_bytes=48 << 20),
        cost_estimate=pl.CostEstimate(
            flops=4 * rows * width * count, bytes_accessed=14 << 20, transcendentals=0
        ),
        name="update",
    )(*arrays)


TURNS = (0, 1, 3, 2)


def moved_along_y(array, turn):
    return lax.ppermute(array, "y", [(i, (i + turn) % 4) for i in range(4)])


def onward_along_y(before, after):
    half = before.shape[0] // 2
    return [moved_along_y(before[:half], 1), moved_along_y(after[half:], 3)]


def joined(own, other, place):
    upper = jnp.where(place == 0, own, other)
    lower = jnp.where(place == 0, other, own)
    return jnp.concatenate([upper, lower], axis=0)


def per_device(precision, samples, step_size, threshold):
    rows_tile, cols_tile = precision.shape
    sample_count = samples.shape[0]
    x, zl, h, zh, y = (lax.axis_index(a) for a in NAMES)
    parts = 8
    piece = sample_count // parts

    block = (x + y) % 4 * 2 + (zl ^ zh)
    mine = lax.dynamic_slice(samples, (block * piece, h * rows_tile), (piece, rows_tile))
    own_eighth = lax.ppermute(mine, NAMES, crossing_of_samples())
    partial = partial_sums(samples, precision)
    shares = lax.all_to_all(partial.reshape(parts, piece, rows_tile), ("y", "zh"), 0, 0, tiled=True)
    own_eighth = own_eighth * jnp.bfloat16(0.5)
    other_eighth = lax.ppermute(own_eighth, "zh", [(0, 1), (1, 0)])
    steps = jnp.stack([step_size[0], step_size[0] * threshold[0]])
    total = jnp.sum(shares.astype(jnp.float32), axis=0)
    projected = total.astype(jnp.bfloat16)
    halved = projected * jnp.bfloat16(0.5)

    crossed = lax.ppermute(projected, NAMES, crossing_of_sums())
    other = lax.ppermute(halved, "zh", [(0, 1), (1, 0)])
    pair = joined(halved, other, zh)
    later, _, pair = lax.optimization_barrier((step_size, threshold, pair))
    row_quarters = [pair, moved_along_y(pair, 1), moved_along_y(pair, 3)]
    own_quarter = joined(own_eighth, other_eighth, zh)
    quarters = [own_quarter, moved_along_y(own_quarter, 1), moved_along_y(own_quarter, 3)]
    quarters += onward_along_y(*quarters[1:])
    row_quarters += onward_along_y(*row_quarters[1:])
    scales = jnp.stack([later[0] * (1.0 / sample_count), later[0]])
    row_start = ((x * 2 + zl) * 2 + h) * rows_tile
    col_start = (zh * 4 + y) * cols_tile
    places_of = [(y - turn) % 4 for turn in TURNS]
    places_of += [(place + zh * 2 + y // 2) % 4 for place in places_of]
    fixed = [row_start, col_start, *places_of]
    own_side = jnp.stack([h, *fixed]).astype(jnp.int32)
    other_side = jnp.stack([1 - h, *fixed]).astype(jnp.int32)
    panel = sent_to_all(crossed, ("x", "zl"), parts).reshape(sample_count, rows_tile)
    other_panel = lax.ppermute(panel, "core", [(0, 1), (1, 0)])
    operands = (scales, steps, row_quarters, quarters, samples)
    half_done = updated_half(own_side, *operands, panel, precision, None)
    return updated_half(other_side, *operands, other_panel, precision, half_done)


def solution(mesh):
    split = Mesh(mesh.devices.reshape(SIZES), NAMES)
    placed = (P(ROW, COL), P(None, COL), P(), P())
    return jax.shard_map(
        per_device, mesh=split, in_specs=placed, out_specs=P(ROW, COL), check_vma=False
    )
```

time: 176 us -> 169 us (0.960)
  waiting for transfers between devices: 76.4 us -> 26.9 us
  starting transfers between devices: 32.3 us -> 67.3 us
  local copies, waits for them, and re-layouts: 2.64 us -> 5.64 us
  Pallas kernels: 25.7 us -> 28.2 us
    all_to_all x1, waiting for transfers between devices: 29.6 us -> 0.42 us  [sent_to_all(): return lax.all_to_all(copies, axes, 0, 0, tiled=True)]
    ppermute x1, starting transfers between devices: 0.29 us -> 29.2 us  [per_device(): other_eighth = lax.ppermute(own_eighth, 'zh', [(0, 1), (1, 0)])]
    ppermute x6 -> x8, waiting for transfers between devices: 35.4 us -> 18.1 us  [moved_along_y(): return lax.ppermute(array, 'y', [(i, (i + turn) % 4) for i in range(4)])]
    ppermute x6 -> x8, starting transfers between devices: 10.4 us -> 19.4 us  [moved_along_y(): return lax.ppermute(array, 'y', [(i, (i + turn) % 4) for i in range(4)])]
    slice x0 -> x4, local copies, waits for them, and re-layouts: none -> 2.91 us  [onward_along_y(): return [moved_along_y(before[:half], 1), moved_along_y(after[half:], 3)]]
    ppermute x1, starting transfers between devices: 3.11 us -> 0.29 us  [per_device(): other = lax.ppermute(halved, 'zh', [(0, 1), (1, 0)])]
    pallas_call x1 -> x2, Pallas kernels: 17.2 us -> 19.7 us  [updated_half(): pl.pallas_call(update_kernel, out_shape=jax.ShapeDtypeStruct(precision.sh...]
  transfers between devices with their start and end apart: 12 -> 14, of which waited for: 8 -> 6; matrix products, arithmetic and copies ran while one was open for 1% -> 3% of each run, Pallas kernels for 0% -> 6%
where the time goes in v5:
time: 169 us; the launch traced here: 168 us
  starting transfers between devices  67.3 us (40%)
  blocking collectives  35.9 us (21%)
  Pallas kernels  28.2 us (17%)
  waiting for transfers between devices  26.9 us (16%)
  local copies, waits for them, and re-layouts  5.64 us (3%)
  other arithmetic  2.24 us (1%)
    all_to_all x1, blocking collectives, per_device(): lax.all_to_all(partial.reshape(parts, piece, rows_tile), ('y', 'zh'), 0,...  35.9 us
    ppermute x1, starting transfers between devices, per_device(): other_eighth = lax.ppermute(own_eighth, 'zh', [(0, 1), (1, 0)])  29.2 us
    pallas_call x2, Pallas kernels, updated_half(): pl.pallas_call(update_kernel, out_shape=jax.ShapeDtypeStruct(precision.sh...  19.7 us
    ppermute x8, starting transfers between devices, moved_along_y(): return lax.ppermute(array, 'y', [(i, (i + turn) % 4) for i in range(4)])  19.4 us
    ppermute x8, waiting for transfers between devices, moved_along_y(): return lax.ppermute(array, 'y', [(i, (i + turn) % 4) for i in range(4)])  18.1 us
    all_to_all x1, starting transfers between devices, sent_to_all(): return lax.all_to_all(copies, axes, 0, 0, tiled=True)  17.1 us
    pallas_call x1, Pallas kernels, partial_sums(): pl.pallas_call(partial_kernel, out_shape=jax.ShapeDtypeStruct((count, row...  8.51 us
    ppermute x1, waiting for transfers between devices, per_device(): other_eighth = lax.ppermute(own_eighth, 'zh', [(0, 1), (1, 0)])  8.34 us
  transfers between devices with their start and end apart: 14, of which 6 were waited for; matrix products, arithmetic and copies ran while one was open for 3% of the time, Pallas kernels for 6%

profile of v5, /device:TPU:0, one launch (start us, length us, event | category | flops | bytes accessed | tf_op | source)
XLA Modules:
  0.0 167.7 jit_solution(13007002541264829824)
XLA Ops:
  0.0 8.5 %partial.1 = bf16[1024,1024]{1,0:T(8,128)(2,1)S(1)} custom-call(bf16[1024,2048]{1,0:T(8,128)(2,1)} %xc.3, f32[1024,2048]{1,0:T(8,128)} %precision.5), custom_call_target="tpu_custom_call" | custom-call | flops 4294967296 | bytes 14680064 | tf_op jit(solution)/shard_map/partial/pallas_call | solution.py:63
  8.5 35.9 %all_to_all.10 = bf16[8,128,1024]{2,1,0:T(8,128)(2,1)} all-to-all(bf16[8,128,1024]{2,1,0:T(8,128)(2,1)S(1)} %bitcast.14), channel_id=1, replica_groups=mesh['x'=4,'zl'=2,'core'=2,'zh'=2,'y'=4] {'y','zh'}, dimensions={0} | all-to-all | bytes 4194304 | tf_op jit(solution)/shard_map/all_to_all | solution.py:193
  44.4 2.0 %reduce_sum.12 = bf16[128,1024]{1,0:T(8,128)(2,1)S(1)} reduce(bf16[8,128,1024]{2,1,0:T(8,128)(2,1)} %all_to_all.10, bf16[]{:T(256)} %constant.103.clone.1), dimensions={0}, to_apply=%region_0.1 | reduce | flops 917504 | bytes 2359298 | tf_op jit(solution)/shard_map/reduce_sum | solution.py:197
  46.4 0.7 collective-permute-start.11
  47.1 0.0 collective-permute-done.11
  47.1 1.6 broadcast_in_dim.2
  48.7 17.1 %all-to-all-start.1 = ((bf16[8,128,1024]{2,1,0:T(8,128)(2,1)}), bf16[8,128,1024]{2,1,0:T(8,128)(2,1)}, u32[]{:S(2)}, u32[]{:S(2)}) async-start(bf16[8,128,1024]{2,1,0:T(8,128)(2,1)} %broadcast_in_dim.2), calls=%async_computation.1 | async-start | bytes 4194304 | tf_op jit(solution)/shard_map/all_to_all | solution.py:42
  65.8 1.0 dynamic_slice.3
  66.8 0.7 collective-permute-start.5
  67.4 0.0 collective-permute-done.5
  67.5 29.2 %collective-permute-start.6 = (bf16[128,1024]{1,0:T(8,128)(2,1)S(1)}, bf16[128,1024]{1,0:T(8,128)(2,1)S(1)}, u32[]{:S(2)}, u32[]{:S(2)}) collective-permute-start(bf16[128,1024]{1,0:T(8,128)(2,1)S(1)} %broadcast_multiply_fusion), channel_id=1, source_target_pairs={{0,4},{4,0},{1,5},{5,1},{2,6},{6,2},{3,7},{7,3},{8,12},{12,8},{9,1... | collective-permute-start | bytes 786440 | tf_op jit(solution)/shard_map/ppermute | solution.py:195
  96.6 0.4 all-to-all-done.1
  97.1 0.0 collective-permute-start.12
  97.1 0.3 collective-permute-start
  97.4 8.3 %collective-permute-done.6 = bf16[128,1024]{1,0:T(8,128)(2,1)S(1)} collective-permute-done((bf16[128,1024]{1,0:T(8,128)(2,1)S(1)}, bf16[128,1024]{1,0:T(8,128)(2,1)S(1)}, u32[]{:S(2)}, u32[]{:S(2)}) %collective-permute-start.6) | collective-permute-done | bytes 262176 | tf_op jit(solution)/shard_map/ppermute | solution.py:195
  105.8 7.7 %collective-permute-start.8 = (bf16[256,1024]{1,0:T(8,128)(2,1)S(1)}, bf16[256,1024]{1,0:T(8,128)(2,1)S(1)}, u32[]{:S(2)}, u32[]{:S(2)}) collective-permute-start(bf16[256,1024]{1,0:T(8,128)(2,1)S(1)} %pad_maximum_fusion.1.x0), channel_id=1, source_target_pairs={{0,3},{1,0},{2,1},{3,2},{4,7},{5,4},{6,5},{7,6},{8,11},{9,8},{10,9... | collective-permute-start | bytes 1572872 | tf_op jit(solution)/shard_map/ppermute | solution.py:168
  113.6 0.0 collective-permute-start.7
  113.6 0.0 collective-permute-done
  113.7 4.3 %collective-permute-start.2 = (bf16[256,1024]{1,0:T(8,128)(2,1)S(1)}, bf16[256,1024]{1,0:T(8,128)(2,1)S(1)}, u32[]{:S(2)}, u32[]{:S(2)}) collective-permute-start(bf16[256,1024]{1,0:T(8,128)(2,1)S(1)} %pad_maximum_fusion.y0), channel_id=1, source_target_pairs={{0,3},{1,0},{2,1},{3,2},{4,7},{5,4},{6,5},{7,6},{8,11},{9,8},{10,9... | collective-permute-start | bytes 1572872 | tf_op jit(solution)/shard_map/ppermute | solution.py:168
  117.9 0.0 collective-permute-start.1
  117.9 5.7 %collective-permute-done.8.x2 = bf16[256,1024]{1,0:T(8,128)(2,1)S(1)} collective-permute-done((bf16[256,1024]{1,0:T(8,128)(2,1)S(1)}, bf16[256,1024]{1,0:T(8,128)(2,1)S(1)}, u32[]{:S(2)}, u32[]{:S(2)}) %collective-permute-start.8) | collective-permute-done | bytes 524320 | tf_op jit(solution)/shard_map/ppermute | solution.py:168
  123.6 0.7 slice.19
  124.4 3.7 %collective-permute-start.10 = (bf16[128,1024]{1,0:T(8,128)(2,1)}, bf16[128,1024]{1,0:T(8,128)(2,1)S(1)}, u32[]{:S(2)}, u32[]{:S(2)}) collective-permute-start(bf16[128,1024]{1,0:T(8,128)(2,1)} %slice.19), channel_id=1, source_target_pairs={{0,3},{1,0},{2,1},{3,2},{4,7},{5,4},{6,5},{7,6},{8,11},{9,8},{10,9... | collective-permute-start | bytes 786440 | tf_op jit(solution)/shard_map/ppermute | solution.py:168
  128.1 0.0 collective-permute-done.7.x1
  128.1 0.7 slice.18
  128.8 0.0 collective-permute-start.9
  128.8 6.1 %collective-permute-done.2.y2 = bf16[256,1024]{1,0:T(8,128)(2,1)S(1)} collective-permute-done((bf16[256,1024]{1,0:T(8,128)(2,1)S(1)}, bf16[256,1024]{1,0:T(8,128)(2,1)S(1)}, u32[]{:S(2)}, u32[]{:S(2)}) %collective-permute-start.2) | collective-permute-done | bytes 524320 | tf_op jit(solution)/shard_map/ppermute | solution.py:168
  134.9 0.7 slice.17
  135.6 3.7 %collective-permute-start.4 = (bf16[128,1024]{1,0:T(8,128)(2,1)}, bf16[128,1024]{1,0:T(8,128)(2,1)}, u32[]{:S(2)}, u32[]{:S(2)}) collective-permute-start(bf16[128,1024]{1,0:T(8,128)(2,1)} %slice.17), channel_id=1, source_target_pairs={{0,3},{1,0},{2,1},{3,2},{4,7},{5,4},{6,5},{7,6},{8,11},{9,8},{10,9... | collective-permute-start | bytes 786440 | tf_op jit(solution)/shard_map/ppermute | solution.py:168
  139.3 0.0 collective-permute-done.1.y1
  139.3 0.7 slice.16
  140.0 0.0 collective-permute-start.3
  141.4 0.1 stack.71.whole
  141.4 0.1 stack.75.whole
  141.5 0.1 pad_maximum_fusion.2
  141.6 0.0 collective-permute-done.10.x4
  141.6 2.1 %collective-permute-done.9.x3 = bf16[128,1024]{1,0:T(8,128)(2,1)} collective-permute-done((bf16[128,1024]{1,0:T(8,128)(2,1)}, bf16[128,1024]{1,0:T(8,128)(2,1)}, u32[]{:S(2)}, u32[]{:S(2)}) %collective-permute-start.9) | collective-permute-done | bytes 262176 | tf_op jit(solution)/shard_map/ppermute | solution.py:168
  143.7 0.0 collective-permute-done.4.y4
  143.7 4.2 %collective-permute-done.3.y3 = bf16[128,1024]{1,0:T(8,128)(2,1)} collective-permute-done((bf16[128,1024]{1,0:T(8,128)(2,1)}, bf16[128,1024]{1,0:T(8,128)(2,1)}, u32[]{:S(2)}, u32[]{:S(2)}) %collective-permute-start.3) | collective-permute-done | bytes 262176 | tf_op jit(solution)/shard_map/ppermute | solution.py:168
  147.9 10.0 %update.2.rest_0_ = f32[1024,2048]{1,0:T(8,128)} custom-call(s32[11]{0:T(128)S(1)} %stack.75.whole, f32[2]{0:T(128)S(1)} %get-tuple-element.13.scales, f32[2]{0:T(128)S(1)} %get-tuple-element.14.steps, bf16[256,1024]{1,0:T(8,128)(2,1)S(1)} %pad_maximum_fusion.y0, bf16[256,1024]{1,0:T(8,128)(2,1)S(1)} %collective-permute-done.1.y1, ...), custom_call_target="tpu_custom_call" | custom-call | flops 4294967296 | bytes 14680064 | tf_op jit(solution)/shard_map/update/pallas_call | solution.py:145
  157.9 0.0 collective-permute-done.12.panel
  157.9 9.7 %update.3 = f32[1024,2048]{1,0:T(8,128)} custom-call(s32[11]{0:T(128)S(1)} %stack.71.whole, f32[2]{0:T(128)S(1)} %get-tuple-element.13.scales, f32[2]{0:T(128)S(1)} %get-tuple-element.14.steps, bf16[256,1024]{1,0:T(8,128)(2,1)S(1)} %pad_maximum_fusion.y0, bf16[256,1024]{1,0:T(8,128)(2,1)S(1)} %collective-permute-done.1.y1, ...), custom_call_target="tpu_custom_call", output_to_operand_aliasing={{}: (16, {})} | custom-call | flops 4294967296 | bytes 14680064 | tf_op jit(solution)/shard_map/update/pallas_call | solution.py:145
  (6 shorter events, 0.2 us)
Async XLA Ops:
  46.4 0.7 collective-permute-start.11
  48.7 48.4 %all-to-all-start.1 = ((bf16[8,128,1024]{2,1,0:T(8,128)(2,1)}), bf16[8,128,1024]{2,1,0:T(8,128)(2,1)}, u32[]{:S(2)}, u32[]{:S(2)}) async-start(bf16[8,128,1024]{2,1,0:T(8,128)(2,1)} %broadcast_in_dim.2), calls=%async_computation.1 | async-start | bytes 4194304 | tf_op jit(solution)/shard_map/all_to_all | solution.py:42
  66.8 0.7 collective-permute-start.5
  67.5 38.2 %collective-permute-start.6 = (bf16[128,1024]{1,0:T(8,128)(2,1)S(1)}, bf16[128,1024]{1,0:T(8,128)(2,1)S(1)}, u32[]{:S(2)}, u32[]{:S(2)}) collective-permute-start(bf16[128,1024]{1,0:T(8,128)(2,1)S(1)} %broadcast_multiply_fusion), channel_id=1, source_target_pairs={{0,4},{4,0},{1,5},{5,1},{2,6},{6,2},{3,7},{7,3},{8,12},{12,8},{9,1... | collective-permute-start | bytes 786440 | tf_op jit(solution)/shard_map/ppermute | solution.py:195
  97.1 60.9 %collective-permute-start.12 = (bf16[1024,1024]{1,0:T(8,128)(2,1)}, bf16[1024,1024]{1,0:T(8,128)(2,1)}, u32[]{:S(2)}, u32[]{:S(2)}) collective-permute-start(bf16[1024,1024]{1,0:T(8,128)(2,1)} %bitcast.12.panel), channel_id=1, source_target_pairs={{0,8},{8,0},{1,9},{9,1},{2,10},{10,2},{3,11},{11,3},{4,12},{12,4},... | collective-permute-start | bytes 6291464 | tf_op jit(solution)/shard_map/ppermute | solution.py:219
  97.1 16.5 %collective-permute-start = (bf16[128,1024]{1,0:T(8,128)(2,1)S(1)}, bf16[128,1024]{1,0:T(8,128)(2,1)S(1)}, u32[]{:S(2)}, u32[]{:S(2)}) collective-permute-start(bf16[128,1024]{1,0:T(8,128)(2,1)S(1)} %broadcast_multiply_fusion.1), channel_id=1, source_target_pairs={{0,4},{4,0},{1,5},{5,1},{2,6},{6,2},{3,7},{7,3},{8,12},{12,8},{9,1... | collective-permute-start | bytes 786440 | tf_op jit(solution)/shard_map/ppermute | solution.py:202
  105.8 17.8 %collective-permute-start.8 = (bf16[256,1024]{1,0:T(8,128)(2,1)S(1)}, bf16[256,1024]{1,0:T(8,128)(2,1)S(1)}, u32[]{:S(2)}, u32[]{:S(2)}) collective-permute-start(bf16[256,1024]{1,0:T(8,128)(2,1)S(1)} %pad_maximum_fusion.1.x0), channel_id=1, source_target_pairs={{0,3},{1,0},{2,1},{3,2},{4,7},{5,4},{6,5},{7,6},{8,11},{9,8},{10,9... | collective-permute-start | bytes 1572872 | tf_op jit(solution)/shard_map/ppermute | solution.py:168
  113.6 14.5 %collective-permute-start.7 = (bf16[256,1024]{1,0:T(8,128)(2,1)S(1)}, bf16[256,1024]{1,0:T(8,128)(2,1)S(1)}, u32[]{:S(2)}, u32[]{:S(2)}) collective-permute-start(bf16[256,1024]{1,0:T(8,128)(2,1)S(1)} %pad_maximum_fusion.1.x0), channel_id=1, source_target_pairs={{0,1},{1,2},{2,3},{3,0},{4,5},{5,6},{6,7},{7,4},{8,9},{9,10},{10,1... | collective-permute-start | bytes 1572872 | tf_op jit(solution)/shard_map/ppermute | solution.py:168
  113.7 21.2 %collective-permute-start.2 = (bf16[256,1024]{1,0:T(8,128)(2,1)S(1)}, bf16[256,1024]{1,0:T(8,128)(2,1)S(1)}, u32[]{:S(2)}, u32[]{:S(2)}) collective-permute-start(bf16[256,1024]{1,0:T(8,128)(2,1)S(1)} %pad_maximum_fusion.y0), channel_id=1, source_target_pairs={{0,3},{1,0},{2,1},{3,2},{4,7},{5,4},{6,5},{7,6},{8,11},{9,8},{10,9... | collective-permute-start | bytes 1572872 | tf_op jit(solution)/shard_map/ppermute | solution.py:168
  117.9 21.4 %collective-permute-start.1 = (bf16[256,1024]{1,0:T(8,128)(2,1)S(1)}, bf16[256,1024]{1,0:T(8,128)(2,1)S(1)}, u32[]{:S(2)}, u32[]{:S(2)}) collective-permute-start(bf16[256,1024]{1,0:T(8,128)(2,1)S(1)} %pad_maximum_fusion.y0), channel_id=1, source_target_pairs={{0,1},{1,2},{2,3},{3,0},{4,5},{5,6},{6,7},{7,4},{8,9},{9,10},{10,1... | collective-permute-start | bytes 1572872 | tf_op jit(solution)/shard_map/ppermute | solution.py:168
  124.4 17.2 %collective-permute-start.10 = (bf16[128,1024]{1,0:T(8,128)(2,1)}, bf16[128,1024]{1,0:T(8,128)(2,1)S(1)}, u32[]{:S(2)}, u32[]{:S(2)}) collective-permute-start(bf16[128,1024]{1,0:T(8,128)(2,1)} %slice.19), channel_id=1, source_target_pairs={{0,3},{1,0},{2,1},{3,2},{4,7},{5,4},{6,5},{7,6},{8,11},{9,8},{10,9... | collective-permute-start | bytes 786440 | tf_op jit(solution)/shard_map/ppermute | solution.py:168
  128.8 14.9 %collective-permute-start.9 = (bf16[128,1024]{1,0:T(8,128)(2,1)}, bf16[128,1024]{1,0:T(8,128)(2,1)}, u32[]{:S(2)}, u32[]{:S(2)}) collective-permute-start(bf16[128,1024]{1,0:T(8,128)(2,1)} %slice.18), channel_id=1, source_target_pairs={{0,1},{1,2},{2,3},{3,0},{4,5},{5,6},{6,7},{7,4},{8,9},{9,10},{10,1... | collective-permute-start | bytes 786440 | tf_op jit(solution)/shard_map/ppermute | solution.py:168
  135.6 8.1 %collective-permute-start.4 = (bf16[128,1024]{1,0:T(8,128)(2,1)}, bf16[128,1024]{1,0:T(8,128)(2,1)}, u32[]{:S(2)}, u32[]{:S(2)}) collective-permute-start(bf16[128,1024]{1,0:T(8,128)(2,1)} %slice.17), channel_id=1, source_target_pairs={{0,3},{1,0},{2,1},{3,2},{4,7},{5,4},{6,5},{7,6},{8,11},{9,8},{10,9... | collective-permute-start | bytes 786440 | tf_op jit(solution)/shard_map/ppermute | solution.py:168
  140.0 7.9 %collective-permute-start.3 = (bf16[128,1024]{1,0:T(8,128)(2,1)}, bf16[128,1024]{1,0:T(8,128)(2,1)}, u32[]{:S(2)}, u32[]{:S(2)}) collective-permute-start(bf16[128,1024]{1,0:T(8,128)(2,1)} %slice.16), channel_id=1, source_target_pairs={{0,1},{1,2},{2,3},{3,0},{4,5},{5,6},{6,7},{7,4},{8,9},{9,10},{10,1... | collective-permute-start | bytes 786440 | tf_op jit(solution)/shard_map/ppermute | solution.py:168
